TPU v7x, 128 devices: a whole 4x4x4 slice. The times are simulated.
128 devices in a mesh: gx: 4 (over x), gy: 8 (over z, core), gz: 4 (over y).
Axes of the slice: x: 4, y: 4, z: 4, core: 2. Of those that a mesh axis runs over, the one named last changes fastest.
Arguments:
- point_data: float32 [128, 128, 7, 32], P(('gx', 'gy', 'gz')), may hold values from -2.8 to 2.8, as said below
- point_cells: int32 [128, 128, 3, 32], P(('gx', 'gy', 'gz')), may hold values from 0 to 127, as said below
- send_counts: int32 [128, 128], P(('gx', 'gy', 'gz')), may hold values from 0 to 32, as said below
Outputs:
- indicator: float32 [64, 128, 512], P('gx', 'gy', 'gz')
- point_values: float32 [128, 128, 32], P(('gx', 'gy', 'gz'))
Inputs may be any that keep to these rules, and one draw needn't show every extreme that they name: `point_data`: channels 0 to 2 of a slot are an oriented normal, channel 3 a confidence between 0.05 and 1, channels 4 to 6 offsets inside the cell between 0 and 1. `point_cells`: channel 0 lies below 16, channel 1 below 16, channel 2 below 128. Slot j from block s to brick d is live where j < send_counts[s, d]. In every draw some brick receives 32 live slots from every block.
All inputs are finite; a program needn't handle non-finite values.
Results may differ from a plain program's by a relative error of at most 0.00002.
Values sent between devices are 32-bit elements; how exact they have to be, the bound alone decides.
A program may use at most 128 MiB of HBM per device.

v0:
```python
import jax
import jax.numpy as jnp
from jax import lax
from jax.sharding import PartitionSpec as P

CX = 16
CY = 16
CZ = 128
ITERS = 6


base_screen = 0.25
point_screen = 4.0


def with_halo(block, sides, width):
    for axis, dim in sides:
        count = lax.axis_size(axis)
        forward = [(i, i + 1) for i in range(count - 1)]
        backward = [(target, source) for source, target in forward]
        low = lax.ppermute(
            lax.slice_in_dim(block, block.shape[dim] - width, None, axis=dim), axis, forward
        )
        high = lax.ppermute(lax.slice_in_dim(block, 0, width, axis=dim), axis, backward)
        block = jnp.concatenate([low, block, high], axis=dim)
    return block


def shifted(shard, axis, by):
    devices = lax.axis_size(axis)
    pairs = [(i, i + by) for i in range(devices) if 0 <= i + by < devices]
    return lax.ppermute(shard, axis, pairs)


def trilinear(offsets, corner_x, corner_y, corner_z):
    along_x = offsets[..., 0, :] if corner_x else 1.0 - offsets[..., 0, :]
    along_y = offsets[..., 1, :] if corner_y else 1.0 - offsets[..., 1, :]
    along_z = offsets[..., 2, :] if corner_z else 1.0 - offsets[..., 2, :]
    return along_x * along_y * along_z


def six_sum(padded):
    total = padded[2:, 1:-1, 1:-1] + padded[:-2, 1:-1, 1:-1]
    total = total + padded[1:-1, 2:, 1:-1] + padded[1:-1, :-2, 1:-1]
    return total + padded[1:-1, 1:-1, 2:] + padded[1:-1, 1:-1, :-2]


def divergence(padded):
    total = padded[0, 2:, 1:-1, 1:-1] - padded[0, :-2, 1:-1, 1:-1]
    total = total + padded[1, 1:-1, 2:, 1:-1] - padded[1, 1:-1, :-2, 1:-1]
    return total + padded[2, 1:-1, 1:-1, 2:] - padded[2, 1:-1, 1:-1, :-2]


def extend(field):
    return with_halo(field, (("gx", 1), ("gy", 2), ("gz", 3)), 1)


def chebyshev(source_term, diagonal, operate):
    half_width = 6.0 / (6.0 + base_screen)
    sigma_ratio = 1.0 / half_width
    rho_prev = half_width
    solution = jnp.zeros_like(source_term)
    residual = source_term
    direction = source_term / diagonal
    for sweep in range(ITERS):
        solution = solution + direction
        residual = residual - operate(direction)
        if sweep + 1 < ITERS:
            rho_next = 1.0 / (2.0 * sigma_ratio - rho_prev)
            direction = (
                rho_next * rho_prev * direction + 2.0 * rho_next / half_width * residual / diagonal
            )
            rho_prev = rho_next
    return solution


def on_device(point_data, point_cells, send_counts):
    slot_count = point_data.shape[3]
    brick_count = point_data.shape[1]
    slot_index = jnp.arange(slot_count, dtype=jnp.int32)
    live_mask = (slot_index[None, None, :] < send_counts[:, :, None]).astype(jnp.float32)
    weight = point_data[:, :, 3, :] * live_mask
    outgoing = jnp.concatenate(
        [point_data[:, :, :3], weight[:, :, None], point_data[:, :, 4:]], axis=2
    )
    got_data, got_cells = (
        lax.all_to_all(outgoing, ("gx", "gy", "gz"), split_axis=1, concat_axis=0, tiled=True),
        lax.all_to_all(point_cells, ("gx", "gy", "gz"), split_axis=1, concat_axis=0, tiled=True),
    )
    got_data = got_data.reshape(brick_count, 7, slot_count)
    got_cells = got_cells.reshape(brick_count, 3, slot_count)
    offsets = got_data[:, 4:7, :]
    got_weight = got_data[:, 3, :]
    cell_x = got_cells[:, 0, :]
    cell_y = got_cells[:, 1, :]
    cell_z = got_cells[:, 2, :]
    volume = jnp.zeros((4, (CX + 1) * (CY + 1) * (CZ + 1)), jnp.float32)
    for corner_x in (0, 1):
        for corner_y in (0, 1):
            for corner_z in (0, 1):
                point_mass = got_weight * trilinear(offsets, corner_x, corner_y, corner_z)
                contrib = jnp.stack(
                    [
                        got_data[:, 0, :] * point_mass,
                        got_data[:, 1, :] * point_mass,
                        got_data[:, 2, :] * point_mass,
                        point_mass,
                    ]
                ).reshape(4, -1)
                linear_at = (
                    ((cell_x + corner_x) * (CY + 1) + cell_y + corner_y) * (CZ + 1)
                    + cell_z
                    + corner_z
                )
                volume = volume.at[:, linear_at.reshape(-1)].add(contrib)
    partial_value = volume.reshape(4, CX + 1, CY + 1, CZ + 1)
    arrived = shifted(partial_value[:, CX], "gx", 1)
    partial_value = partial_value[:, :CX].at[:, 0].add(arrived)
    arrived = shifted(partial_value[:, :, CY], "gy", 1)
    partial_value = partial_value[:, :, :CY].at[:, :, 0].add(arrived)
    arrived = shifted(partial_value[:, :, :, CZ], "gz", 1)
    splat = partial_value[:, :, :, :CZ].at[:, :, :, 0].add(arrived)
    source_term = -0.5 * divergence(extend(splat[:3]))
    diagonal = 6.0 + base_screen + point_screen * splat[3]

    def operate(field):
        return diagonal * field - six_sum(extend(field[None])[0])

    indicator = chebyshev(source_term, diagonal, operate)
    extended = extend(indicator[None])[0]
    extended = extended.reshape(-1)
    values = jnp.zeros(got_weight.shape, jnp.float32)
    for corner_x in (0, 1):
        for corner_y in (0, 1):
            for corner_z in (0, 1):
                linear_at = (
                    ((cell_x + 1 + corner_x) * (CY + 2) + cell_y + 1 + corner_y) * (CZ + 2)
                    + cell_z
                    + 1
                    + corner_z
                )
                values = (
                    values + trilinear(offsets, corner_x, corner_y, corner_z) * extended[linear_at]
                )
    returned = lax.all_to_all(
        values.reshape(brick_count, 1, slot_count),
        ("gx", "gy", "gz"),
        split_axis=0,
        concat_axis=1,
        tiled=True,
    )
    point_values = returned * live_mask
    return (indicator, point_values)


def solution(mesh):
    in_specs = (
        P(("gx", "gy", "gz"), None, None, None),
        P(("gx", "gy", "gz"), None, None, None),
        P(("gx", "gy", "gz"), None),
    )
    out_specs = (P("gx", "gy", "gz"), P(("gx", "gy", "gz"), None, None))
    return jax.shard_map(
        on_device, mesh=mesh, in_specs=in_specs, out_specs=out_specs, check_vma=False
    )
```

profile of v0, /device:TPU:1, one launch (start us, length us, event | category | flops | bytes accessed | tf_op | source)
XLA Modules:
  0.0 740.0 jit_solution(17908838230578275254)
XLA Ops:
  2.3 11.5 %all-to-all-start = ((s32[1,128,3,32]{3,2,0,1:T(4,128)}), s32[1,128,3,32]{3,2,0,1:T(4,128)S(1)}, u32[]{:S(2)}, u32[]{:S(2)}) async-start(s32[1,128,3,32]{3,2,0,1:T(4,128)} %copy.141), calls=%async_computation | async-start | bytes 524288 | tf_op jit(solution)/shard_map/all_to_all | solution.py:88
  19.1 5.9 all-to-all-done
  25.1 3.9 all-to-all-start.1
  30.1 8.9 %all-to-all-done.1 = f32[128,1,224]{2,1,0:T(1,128)S(1)} async-done(((f32[128,1,224]{2,1,0:T(1,128)}), f32[128,1,224]{2,1,0:T(1,128)S(1)}, u32[]{:S(2)}, u32[]{:S(2)}) %all-to-all-start.1) | async-done | bytes 114720 | tf_op jit(solution)/shard_map/all_to_all | solution.py:87
  57.6 30.5 %scatter_custom_fusion = f32[4,37281]{0,1:T(8,128)} fusion(s32[4096]{0:T(1024)S(1)} %bitcast.221, f32[4096,4]{1,0:T(8,128)} %copy.146, f32[]{:T(128)} %constant.121.clone.1), kind=kCustom, calls=%fused_computation.16 | custom fusion | flops 16384 | bytes 597008 | tf_op jit(solution)/shard_map/scatter-add | solution.py:115
  88.1 33.0 %scatter_fusion = f32[4,37281]{0,1:T(8,128)} fusion(f32[4,37281]{0,1:T(8,128)} %scatter_custom_fusion, s32[4096]{0:T(1024)S(1)} %bitcast.214, f32[4096,4]{1,0:T(8,128)S(1)} %copy.147), kind=kCustom, calls=%fused_computation.9 | custom fusion | flops 16384 | bytes 212992 | tf_op jit(solution)/shard_map/scatter-add | solution.py:115
  121.1 33.3 %scatter_fusion.1 = f32[4,37281]{0,1:T(8,128)} fusion(f32[4,37281]{0,1:T(8,128)} %scatter_fusion, s32[4096]{0:T(1024)S(1)} %bitcast.217, f32[4096,4]{1,0:T(8,128)} %copy.149), kind=kCustom, calls=%fused_computation.10 | custom fusion | flops 16384 | bytes 212992 | tf_op jit(solution)/shard_map/scatter-add | solution.py:115
  154.4 33.3 %scatter_fusion.2 = f32[4,37281]{0,1:T(8,128)} fusion(f32[4,37281]{0,1:T(8,128)} %scatter_fusion.1, s32[4096]{0:T(1024)S(1)} %bitcast.213, f32[4096,4]{1,0:T(8,128)} %copy.150), kind=kCustom, calls=%fused_computation.11 | custom fusion | flops 16384 | bytes 212992 | tf_op jit(solution)/shard_map/scatter-add | solution.py:115
  187.7 33.3 %scatter_fusion.3 = f32[4,37281]{0,1:T(8,128)} fusion(f32[4,37281]{0,1:T(8,128)} %scatter_fusion.2, s32[4096]{0:T(1024)S(1)} %bitcast.215, f32[4096,4]{1,0:T(8,128)} %copy.152), kind=kCustom, calls=%fused_computation.12 | custom fusion | flops 16384 | bytes 212992 | tf_op jit(solution)/shard_map/scatter-add | solution.py:115
  221.0 33.5 %scatter_fusion.4 = f32[4,37281]{0,1:T(8,128)} fusion(f32[4,37281]{0,1:T(8,128)} %scatter_fusion.3, s32[4096]{0:T(1024)S(1)} %bitcast.211, f32[4096,4]{1,0:T(8,128)} %copy.153), kind=kCustom, calls=%fused_computation.13 | custom fusion | flops 16384 | bytes 212992 | tf_op jit(solution)/shard_map/scatter-add | solution.py:115
  254.5 33.3 %scatter_fusion.5 = f32[4,37281]{0,1:T(8,128)} fusion(f32[4,37281]{0,1:T(8,128)} %scatter_fusion.4, s32[4096]{0:T(1024)S(1)} %bitcast.216, f32[4096,4]{1,0:T(8,128)} %copy.155), kind=kCustom, calls=%fused_computation.14 | custom fusion | flops 16384 | bytes 212992 | tf_op jit(solution)/shard_map/scatter-add | solution.py:115
  287.8 33.3 %scatter_fusion.6 = f32[4,37281]{0,1:T(8,128)} fusion(f32[4,37281]{0,1:T(8,128)} %scatter_fusion.5, s32[4096]{0:T(1024)S(1)} %bitcast.212, f32[4096,4]{1,0:T(8,128)} %copy.156), kind=kCustom, calls=%fused_computation.15 | custom fusion | flops 16384 | bytes 212992 | tf_op jit(solution)/shard_map/scatter-add | solution.py:115
  321.2 10.8 %copy.157 = f32[4,37281]{1,0:T(4,128)S(1)} copy(f32[4,37281]{0,1:T(8,128)} %scatter_fusion.6) | data formatting | bytes 1192992 | tf_op jit(solution)/shard_map/scatter-add | solution.py:115
  336.7 3.5 collective-permute-start.1
  348.8 4.7 collective-permute-start.4
  356.9 5.5 collective-permute-start.6
  365.8 4.6 collective-permute-start.8
  373.3 4.6 collective-permute-start.9
  378.7 5.9 collective-permute-start.11
  386.6 3.0 collective-permute-done.12
  389.8 3.9 collective-permute-start.13
  397.5 4.1 collective-permute-done.14
  402.2 3.9 collective-permute-start.15
  407.4 3.4 collective-permute-done.16
  410.8 5.6 collective-permute-start.17
  418.4 3.0 collective-permute-done.18
  421.6 3.4 collective-permute-start.19
  428.7 4.1 collective-permute-done.20
  433.4 3.6 collective-permute-start.21
  438.4 3.7 collective-permute-done.22
  442.1 5.0 collective-permute-start.23
  458.1 4.4 collective-permute-done.26
  463.0 3.6 collective-permute-start.27
  471.1 3.8 collective-permute-start.29
  485.7 4.1 collective-permute-done.32
  496.5 3.6 collective-permute-start.35
  511.0 4.1 collective-permute-done.38
  521.7 3.6 collective-permute-start.41
  535.9 4.1 collective-permute-done.44
  540.5 23.0 %gather_fusion.3 = f32[4096]{0:T(1024)S(1)} fusion(f32[42120]{0:T(1024)S(1)} %reshape_squeeze.3, s32[4096]{0:T(1024)S(1)} %broadcast_clamp_fusion.4), kind=kCustom, calls=%fused_computation.3 | custom fusion | bytes 49152 | tf_op jit(solution)/shard_map/gather | solution.py:143
  563.7 23.0 %gather_fusion.2 = f32[4096]{0:T(1024)S(1)} fusion(f32[42120]{0:T(1024)S(1)} %reshape_squeeze.3, s32[4096]{0:T(1024)S(1)} %broadcast_clamp_fusion.5), kind=kCustom, calls=%fused_computation.2 | custom fusion | bytes 49152 | tf_op jit(solution)/shard_map/gather | solution.py:143
  586.8 23.0 %gather_fusion = f32[4096]{0:T(1024)S(1)} fusion(f32[42120]{0:T(1024)S(1)} %reshape_squeeze.3, s32[4096]{0:T(1024)S(1)} %broadcast_clamp_fusion.7), kind=kCustom, calls=%fused_computation | custom fusion | bytes 49152 | tf_op jit(solution)/shard_map/gather | solution.py:143
  609.9 23.0 %gather_fusion.5 = f32[4096]{0:T(1024)S(1)} fusion(f32[42120]{0:T(1024)S(1)} %reshape_squeeze.3, s32[4096]{0:T(1024)S(1)} %broadcast_clamp_fusion.2), kind=kCustom, calls=%fused_computation.5 | custom fusion | bytes 49152 | tf_op jit(solution)/shard_map/gather | solution.py:143
  633.0 23.0 %gather_fusion.1 = f32[4096]{0:T(1024)S(1)} fusion(f32[42120]{0:T(1024)S(1)} %reshape_squeeze.3, s32[4096]{0:T(1024)S(1)} %broadcast_clamp_fusion.6), kind=kCustom, calls=%fused_computation.1 | custom fusion | bytes 49152 | tf_op jit(solution)/shard_map/gather | solution.py:143
  656.1 23.0 %gather_fusion.4 = f32[4096]{0:T(1024)S(1)} fusion(f32[42120]{0:T(1024)S(1)} %reshape_squeeze.3, s32[4096]{0:T(1024)S(1)} %broadcast_clamp_fusion.3), kind=kCustom, calls=%fused_computation.4 | custom fusion | bytes 49152 | tf_op jit(solution)/shard_map/gather | solution.py:143
  679.2 23.0 %gather_fusion.6 = f32[4096]{0:T(1024)S(1)} fusion(f32[42120]{0:T(1024)S(1)} %reshape_squeeze.3, s32[4096]{0:T(1024)S(1)} %broadcast_clamp_fusion.1), kind=kCustom, calls=%fused_computation.6 | custom fusion | bytes 49152 | tf_op jit(solution)/shard_map/gather | solution.py:143
  702.4 23.0 %gather_fusion.7 = f32[4096]{0:T(1024)S(1)} fusion(f32[42120]{0:T(1024)S(1)} %reshape_squeeze.3, s32[4096]{0:T(1024)S(1)} %broadcast_clamp_fusion), kind=kCustom, calls=%fused_computation.7 | custom fusion | bytes 49152 | tf_op jit(solution)/shard_map/gather | solution.py:143
  726.5 12.4 %all_to_all.30 = f32[128,1,32]{2,1,0:T(1,128)S(1)} all-to-all(f32[128,1,32]{2,1,0:T(1,128)S(1)} %bitcast.209), channel_id=1, replica_groups=mesh['gx'=4,'gy'=8,'gz'=4] {'gx','gy','gz'}, dimensions={0} | all-to-all | bytes 32768 | tf_op jit(solution)/shard_map/all_to_all | solution.py:145
  (214 shorter events, 129.6 us)
Async XLA Ops:
  2.3 22.8 %all-to-all-start = ((s32[1,128,3,32]{3,2,0,1:T(4,128)}), s32[1,128,3,32]{3,2,0,1:T(4,128)S(1)}, u32[]{:S(2)}, u32[]{:S(2)}) async-start(s32[1,128,3,32]{3,2,0,1:T(4,128)} %copy.141), calls=%async_computation | async-start | bytes 524288 | tf_op jit(solution)/shard_map/all_to_all | solution.py:88
  25.1 13.9 %all-to-all-start.1 = ((f32[128,1,224]{2,1,0:T(1,128)}), f32[128,1,224]{2,1,0:T(1,128)S(1)}, u32[]{:S(2)}, u32[]{:S(2)}) async-start(f32[128,1,224]{2,1,0:T(1,128)} %reshape.2101), calls=%async_computation.1 | async-start | bytes 262144 | tf_op jit(solution)/shard_map/all_to_all | solution.py:87
  332.8 3.8 collective-permute-start
  336.7 4.8 collective-permute-start.1
  342.6 3.3 collective-permute-start.2
  347.5 6.1 collective-permute-start.3
  348.8 5.7 collective-permute-start.4
  354.5 7.9 %collective-permute-start.5 = (f32[3,18,1,128]{3,2,1,0:T(1,128)S(1)}, f32[3,18,1,128]{3,2,1,0:T(1,128)S(1)}, u32[]{:S(2)}, u32[]{:S(2)}) collective-permute-start(f32[3,18,1,128]{3,2,1,0:T(1,128)S(1)} %get-tuple-element.90), channel_id=1, source_target_pairs={{4,0},{8,4},{12,8},{16,12},{20,16},{24,20},{28,24},{5,1},{9,5},{13... | collective-permute-start | bytes 82952 | tf_op jit(solution)/shard_map/ppermute | solution.py:24
  356.9 6.5 collective-permute-start.6
  364.1 6.3 collective-permute-start.7
  365.8 5.5 collective-permute-start.8
  372.0 5.9 collective-permute-start.10
  373.3 5.3 collective-permute-start.9
  378.7 7.9 %collective-permute-start.11 = (f32[1,18,1,128]{3,2,1,0:T(1,128)S(1)}, f32[1,18,1,128]{3,2,1,0:T(1,128)S(1)}, u32[]{:S(2)}, u32[]{:S(2)}) collective-permute-start(f32[1,18,1,128]{3,2,1,0:T(1,128)S(1)} %get-tuple-element.113), channel_id=1, source_target_pairs={{0,4},{4,8},{8,12},{12,16},{16,20},{20,24},{24,28},{1,5},{5,9},{9,... | collective-permute-start | bytes 27656 | tf_op jit(solution)/shard_map/ppermute | solution.py:21
  384.6 5.0 collective-permute-start.12
  389.8 7.7 %collective-permute-start.13 = (f32[1,18,18,1]{3,2,1,0:T(8,128)S(1)}, f32[1,18,18,1]{3,2,1,0:T(8,128)S(1)}, u32[]{:S(2)}, u32[]{:S(2)}) collective-permute-start(f32[1,18,18,1]{3,2,1,0:T(8,128)S(1)} %get-tuple-element.101), channel_id=1, source_target_pairs={{0,1},{1,2},{2,3},{4,5},{5,6},{6,7},{8,9},{9,10},{10,11},{12,13},{... | collective-permute-start | bytes 3896 | tf_op jit(solution)/shard_map/ppermute | solution.py:21
  393.7 7.9 %collective-permute-start.14 = (f32[1,18,18,1]{3,2,1,0:T(8,128)S(1)}, f32[1,18,18,1]{3,2,1,0:T(8,128)S(1)}, u32[]{:S(2)}, u32[]{:S(2)}) collective-permute-start(f32[1,18,18,1]{3,2,1,0:T(8,128)S(1)} %get-tuple-element.102), channel_id=1, source_target_pairs={{1,0},{2,1},{3,2},{5,4},{6,5},{7,6},{9,8},{10,9},{11,10},{13,12},{... | collective-permute-start | bytes 3896 | tf_op jit(solution)/shard_map/ppermute | solution.py:24
  402.2 5.2 collective-permute-start.15
  406.1 4.7 collective-permute-start.16
  410.8 7.5 %collective-permute-start.17 = (f32[1,18,1,128]{3,2,1,0:T(1,128)S(1)}, f32[1,18,1,128]{3,2,1,0:T(1,128)S(1)}, u32[]{:S(2)}, u32[]{:S(2)}) collective-permute-start(f32[1,18,1,128]{3,2,1,0:T(1,128)S(1)} %get-tuple-element.111), channel_id=1, source_target_pairs={{0,4},{4,8},{8,12},{12,16},{16,20},{20,24},{24,28},{1,5},{5,9},{9,... | collective-permute-start | bytes 27656 | tf_op jit(solution)/shard_map/ppermute | solution.py:21
  416.4 5.0 collective-permute-start.18
  421.6 7.2 collective-permute-start.19
  424.9 7.9 %collective-permute-start.20 = (f32[1,18,18,1]{3,2,1,0:T(8,128)S(1)}, f32[1,18,18,1]{3,2,1,0:T(8,128)S(1)}, u32[]{:S(2)}, u32[]{:S(2)}) collective-permute-start(f32[1,18,18,1]{3,2,1,0:T(8,128)S(1)} %get-tuple-element.100), channel_id=1, source_target_pairs={{1,0},{2,1},{3,2},{5,4},{6,5},{7,6},{9,8},{10,9},{11,10},{13,12},{... | collective-permute-start | bytes 3896 | tf_op jit(solution)/shard_map/ppermute | solution.py:24
  433.4 4.9 collective-permute-start.21
  437.1 5.0 collective-permute-start.22
  442.1 6.9 collective-permute-start.23
  447.1 5.0 collective-permute-start.24
  452.3 5.8 collective-permute-start.25
  454.6 7.9 %collective-permute-start.26 = (f32[1,18,18,1]{3,2,1,0:T(8,128)S(1)}, f32[1,18,18,1]{3,2,1,0:T(8,128)S(1)}, u32[]{:S(2)}, u32[]{:S(2)}) collective-permute-start(f32[1,18,18,1]{3,2,1,0:T(8,128)S(1)} %get-tuple-element.98), channel_id=1, source_target_pairs={{1,0},{2,1},{3,2},{5,4},{6,5},{7,6},{9,8},{10,9},{11,10},{13,12},{... | collective-permute-start | bytes 3896 | tf_op jit(solution)/shard_map/ppermute | solution.py:24
  463.0 5.2 collective-permute-start.27
  466.7 4.4 collective-permute-start.28
  471.1 5.9 collective-permute-start.29
  474.9 5.0 collective-permute-start.30
  480.0 5.7 collective-permute-start.31
  482.0 7.9 %collective-permute-start.32 = (f32[1,18,18,1]{3,2,1,0:T(8,128)S(1)}, f32[1,18,18,1]{3,2,1,0:T(8,128)S(1)}, u32[]{:S(2)}, u32[]{:S(2)}) collective-permute-start(f32[1,18,18,1]{3,2,1,0:T(8,128)S(1)} %get-tuple-element.96), channel_id=1, source_target_pairs={{1,0},{2,1},{3,2},{5,4},{6,5},{7,6},{9,8},{10,9},{11,10},{13,12},{... | collective-permute-start | bytes 3896 | tf_op jit(solution)/shard_map/ppermute | solution.py:24
  490.4 3.1 collective-permute-start.33
  492.1 4.4 collective-permute-start.34
  496.5 5.7 collective-permute-start.35
  500.1 5.0 collective-permute-start.36
  505.2 5.7 collective-permute-start.37
  507.2 7.9 %collective-permute-start.38 = (f32[1,18,18,1]{3,2,1,0:T(8,128)S(1)}, f32[1,18,18,1]{3,2,1,0:T(8,128)S(1)}, u32[]{:S(2)}, u32[]{:S(2)}) collective-permute-start(f32[1,18,18,1]{3,2,1,0:T(8,128)S(1)} %get-tuple-element.94), channel_id=1, source_target_pairs={{1,0},{2,1},{3,2},{5,4},{6,5},{7,6},{9,8},{10,9},{11,10},{13,12},{... | collective-permute-start | bytes 3896 | tf_op jit(solution)/shard_map/ppermute | solution.py:24
  515.6 48.0 %copy-start.1 = (f32[16,16,128]{2,1,0:T(8,128)}, f32[16,16,128]{2,1,0:T(8,128)S(1)}, u32[]{:S(2)}) copy-start(f32[16,16,128]{2,1,0:T(8,128)S(1)} %fusion.7) | copy-start | bytes 393220
  515.7 3.1 collective-permute-start.39
  517.3 4.4 collective-permute-start.40
  521.7 5.7 collective-permute-start.41
  525.3 5.0 collective-permute-start.42
  530.5 5.4 collective-permute-start.43
  532.1 7.9 %collective-permute-start.44 = (f32[1,18,18,1]{3,2,1,0:T(8,128)S(1)}, f32[1,18,18,1]{3,2,1,0:T(8,128)S(1)}, u32[]{:S(2)}, u32[]{:S(2)}) collective-permute-start(f32[1,18,18,1]{3,2,1,0:T(8,128)S(1)} %get-tuple-element.92), channel_id=1, source_target_pairs={{1,0},{2,1},{3,2},{5,4},{6,5},{7,6},{9,8},{10,9},{11,10},{13,12},{... | collective-permute-start | bytes 3896 | tf_op jit(solution)/shard_map/ppermute | solution.py:24
  (2 other events, 37.3 us)
where the time goes:
time: 750 us; the launch traced here: 740 us
  other arithmetic  273 us (36%)
  local copies, waits for them, and re-layouts  226 us (30%)
  starting transfers between devices  132 us (18%)
  waiting for transfers between devices  94.1 us (13%)
  blocking collectives  12.4 us (2%)
    scatter-add x8, other arithmetic, on_device(): volume = volume.at[:, linear_at.reshape(-1)].add(contrib)  264 us
    gather x16, local copies, waits for them, and re-layouts, on_device(): extended[linear_at]  185 us
    ppermute x21, starting transfers between devices, with_halo(): lax.ppermute(lax.slice_in_dim(block, block.shape[dim] - width, None, axis...  76.4 us
    ppermute x21, waiting for transfers between devices, with_halo(): lax.ppermute(lax.slice_in_dim(block, 0, width, axis=dim), axis, backward)  58.3 us
    ppermute x21, starting transfers between devices, with_halo(): lax.ppermute(lax.slice_in_dim(block, 0, width, axis=dim), axis, backward)  32 us
    ppermute x21, waiting for transfers between devices, with_halo(): lax.ppermute(lax.slice_in_dim(block, block.shape[dim] - width, None, axis...  17.3 us
  transfers between devices with their start and end apart: 47, of which 32 were waited for; matrix products, arithmetic and copies ran while one was open for 1% of the time, Pallas kernels for 0%

commit v1 on v0

v1 whole, which is shorter than its diff:
```python
import functools

import jax
import jax.numpy as jnp
from jax import lax
from jax.experimental import pallas as pl
from jax.experimental.pallas import tpu as pltpu
from jax.sharding import PartitionSpec as P

MESH = pl.DeviceIdType.MESH
F32 = jnp.float32
BF16 = jnp.bfloat16

DEVICES = 128
CAP = 32
CHANNELS = 10
WIDTH = 384
POINTS = 512
ROWS = 304
ITERS = 6

base_screen = 0.25
point_screen = 4.0


def sweep_factors():
    half_width = 6.0 / (6.0 + base_screen)
    rho_prev = half_width
    factors = []
    for _ in range(ITERS - 1):
        rho_next = 1.0 / (2.0 / half_width - rho_prev)
        factors.append((rho_next * rho_prev, 2.0 * rho_next / half_width))
        rho_prev = rho_next
    return factors


def position(sizes):
    return tuple(lax.axis_index(name) for name in ("gx", "gy", "gz"))


def coordinates(sizes, index):
    ny, nz = sizes[1], sizes[2]
    return (index // (ny * nz), lax.rem(index // nz, ny), lax.rem(index, nz))


def vmem():
    return pl.BlockSpec(memory_space=pltpu.VMEM)


def greet_all(sizes, me):
    barrier = pltpu.get_barrier_semaphore()

    @pl.loop(1, DEVICES)
    def _(step):
        other = lax.rem(me + step, DEVICES)
        pl.semaphore_signal(barrier, inc=1, device_id=coordinates(sizes, other), device_id_type=MESH)


def exchange_rows(sizes, me, send, recv, sent, send_sem, recv_sem):
    pl.semaphore_wait(pltpu.get_barrier_semaphore(), DEVICES - 1)

    @pl.loop(1, DEVICES)
    def _(step):
        other = lax.rem(me + step, DEVICES)
        pltpu.make_async_remote_copy(
            src_ref=send.at[pl.ds(other, 1)],
            dst_ref=recv.at[pl.ds(me, 1)],
            send_sem=send_sem,
            recv_sem=recv_sem,
            device_id=coordinates(sizes, other),
            device_id_type=MESH,
        ).start()

    pltpu.make_async_copy(send.at[pl.ds(me, 1)], recv.at[pl.ds(me, 1)], recv_sem).start()
    pltpu.make_async_copy(send.at[pl.ds(me, 1)], sent, send_sem).start()
    pltpu.make_async_copy(send, recv, send_sem).wait()
    pltpu.make_async_copy(send, recv, recv_sem).wait()


def route_kernel(sizes, data_ref, cells_ref, counts_ref, out_ref, send, recv, sent, send_sem, recv_sem):
    gx, gy, gz = position(sizes)
    me = (gx * sizes[1] + gy) * sizes[2] + gz
    greet_all(sizes, me)
    slot = lax.broadcasted_iota(jnp.int32, (CAP, DEVICES), 0)
    weight = jnp.where(slot < counts_ref[...], data_ref[3], 0.0)
    parts = [data_ref[c] * weight for c in range(3)] + [weight]
    parts += [data_ref[4 + c] for c in range(3)] + [cells_ref[c].astype(F32) for c in range(3)]
    parts += [jnp.zeros((WIDTH - CAP * CHANNELS, DEVICES), F32)]
    send[...] = jnp.concatenate(parts, axis=0).T
    exchange_rows(sizes, me, send, recv, sent, send_sem, recv_sem)
    out_ref[...] = recv[...].T[: CAP * CHANNELS].reshape(CHANNELS, CAP, DEVICES)


def return_kernel(sizes, values_ref, counts_ref, out_ref, send, recv, sent, send_sem, recv_sem):
    gx, gy, gz = position(sizes)
    me = (gx * sizes[1] + gy) * sizes[2] + gz
    greet_all(sizes, me)
    padded = jnp.concatenate([values_ref[...], jnp.zeros((DEVICES - CAP, DEVICES), F32)], axis=0)
    send[...] = padded.T
    exchange_rows(sizes, me, send, recv, sent, send_sem, recv_sem)
    slot = lax.broadcasted_iota(jnp.int32, (CAP, DEVICES), 0)
    out_ref[...] = jnp.where(slot < counts_ref[...], recv[...].T[:CAP], 0.0)


def split(value):
    high = value.astype(BF16)
    return high, (value - high.astype(F32)).astype(BF16)


def point_rows(d_ref, group, channel):
    count = POINTS // DEVICES
    rows = [d_ref[channel, pl.ds(group * count + q, 1), :] for q in range(count)]
    return jnp.concatenate(rows, axis=1)


def spread(row):
    return jnp.broadcast_to(row, (16, POINTS)).astype(BF16)


def spread_split(row):
    wide = jnp.broadcast_to(row, (16, POINTS))
    return split(wide)


def splat_kernel(d_ref, acc_ref, ov_ref, a_ref, b_ref):
    acc_ref[...] = jnp.zeros_like(acc_ref)
    ov_ref[...] = jnp.zeros_like(ov_ref)
    iota = lax.broadcasted_iota(jnp.int32, (16, POINTS), 0).astype(F32).astype(BF16)
    zero = jnp.zeros((16, POINTS), BF16)

    def store_a(first, high, low):
        rows = pl.ds(first, 16)
        a_ref[rows, 0:POINTS] = high
        a_ref[rows, POINTS : 2 * POINTS] = low
        a_ref[rows, 2 * POINTS : 3 * POINTS] = high

    def store_b(first, high, low):
        rows = pl.ds(first, 16)
        b_ref[rows, 0:POINTS] = high
        b_ref[rows, POINTS : 2 * POINTS] = high
        b_ref[rows, 2 * POINTS : 3 * POINTS] = low

    @pl.loop(0, CAP * DEVICES // POINTS)
    def _(group):
        v = [point_rows(d_ref, group, c) for c in range(4)]
        fx, fy, fz, cx, cy, cz = [point_rows(d_ref, group, 4 + c) for c in range(6)]
        bx, by, bz = spread(cx), spread(cy), spread(cz)
        y0, y1 = by == iota, (by + 1.0).astype(BF16) == iota
        near = [], []
        for along, out in ((1.0 - fx, 0), (fx, 1)):
            w0 = spread_split(along * (1.0 - fy))
            w1 = spread_split(along * fy)
            for part in range(2):
                near[out].append(jnp.where(y0, w0[part], jnp.where(y1, w1[part], zero)))
        for x in range(17):
            x0, x1 = bx == x, bx == x - 1
            high, low = [jnp.where(x0, near[0][part], jnp.where(x1, near[1][part], zero)) for part in range(2)]
            store_a(16 * x, high, low)
        edge = jnp.where(cy == 15.0, fy, 0.0)
        e0, e1 = spread_split((1.0 - fx) * edge), spread_split(fx * edge)
        for t in range(2):
            at = iota + jnp.asarray(16 * t, BF16)
            x0, x1 = bx == at, (bx + 1.0).astype(BF16) == at
            high, low = [jnp.where(x0, e0[part], jnp.where(x1, e1[part], zero)) for part in range(2)]
            store_a(272 + 16 * t, high, low)
        g0 = [spread_split(v[c] * (1.0 - fz)) for c in range(4)]
        g1 = [spread_split(v[c] * fz) for c in range(4)]
        for t in range(8):
            at = iota + jnp.asarray(16 * t, BF16)
            z0, z1 = bz == at, (bz + 1.0).astype(BF16) == at
            for c in range(4):
                high, low = [jnp.where(z0, g0[c][part], jnp.where(z1, g1[c][part], zero)) for part in range(2)]
                store_b(128 * c + 16 * t, high, low)
        top = bz == 127
        high, low = zero, zero
        for c in range(4):
            here = jnp.logical_and(top, iota == c)
            high, low = jnp.where(here, g1[c][0], high), jnp.where(here, g1[c][1], low)
        store_b(512, high, low)
        dims = (((1,), (1,)), ((), ()))
        acc_ref[...] += lax.dot_general(a_ref[...], b_ref[0:512, :], dims, preferred_element_type=F32)
        ov_ref[:, 0:16] += lax.dot_general(a_ref[...], b_ref[512:528, :], dims, preferred_element_type=F32)


def interp_kernel(d_ref, u_ref, halo_ref, uz_ref, out_ref, l_ref, r_ref):
    for first, source in ((0, u_ref), (256, halo_ref)):
        value = source[...]
        rows = pl.ds(first, value.shape[0])
        high, low = split(value)
        l_ref[rows, 0:128] = high
        l_ref[rows, 128:256] = low
        l_ref[rows, 256:384] = high
    top = jnp.broadcast_to(uz_ref[:, 0:1], (ROWS, 128))
    high = top.astype(BF16).astype(F32)
    lane = lax.broadcasted_iota(jnp.int32, (ROWS, 128), 1)
    low = jnp.where(lane == 1, top - high, 0.0)
    l_ref[:, 384:512] = jnp.where(jnp.logical_or(lane == 0, lane == 2), high, low).astype(BF16)
    r_ref[400:512, :] = jnp.zeros((112, POINTS), BF16)
    iota_f = lax.broadcasted_iota(jnp.int32, (16, POINTS), 0).astype(F32)
    iota = iota_f.astype(BF16)
    zero = jnp.zeros((16, POINTS), BF16)

    @pl.loop(0, CAP * DEVICES // POINTS)
    def _(group):
        fx, fy, fz, cx, cy, cz = [point_rows(d_ref, group, 4 + c) for c in range(6)]
        bz = spread(cz)
        g0, g1 = spread_split(1.0 - fz), spread_split(fz)
        for t in range(8):
            at = iota + jnp.asarray(16 * t, BF16)
            z0, z1 = bz == at, (bz + 1.0).astype(BF16) == at
            high, low = [jnp.where(z0, g0[part], jnp.where(z1, g1[part], zero)) for part in range(2)]
            r_ref[pl.ds(16 * t, 16), :] = high
            r_ref[pl.ds(128 + 16 * t, 16), :] = high
            r_ref[pl.ds(256 + 16 * t, 16), :] = low
        top = bz == 127
        high = jnp.where(jnp.logical_and(top, iota <= 1), g1[0], zero)
        r_ref[384:400, :] = jnp.where(jnp.logical_and(top, iota == 2), g1[1], high)
        g = jnp.dot(l_ref[...], r_ref[...], preferred_element_type=F32)
        total = jnp.zeros((16, POINTS), F32)
        for x in range(17):
            hat = jnp.where(cx == x, 1.0 - fx, jnp.where(cx == x - 1, fx, 0.0))
            total = total + hat * g[16 * x : 16 * x + 16]
        hat = jnp.where(cy == iota_f, 1.0 - fy, jnp.where(cy + 1.0 == iota_f, fy, 0.0))
        total = total * hat
        edge = jnp.where(cy == 15.0, fy, 0.0)
        for t in range(2):
            at = iota_f + 16.0 * t
            hat = jnp.where(cx == at, 1.0 - fx, jnp.where(cx + 1.0 == at, fx, 0.0))
            total = total + hat * edge * g[272 + 16 * t : 288 + 16 * t]
        value = jnp.sum(total, axis=0, keepdims=True)
        count = POINTS // DEVICES
        for q in range(count):
            out_ref[pl.ds(group * count + q, 1), :] = value[:, q * DEVICES : (q + 1) * DEVICES]


def roll_to(tile, source, target):
    shift = (target - source) % 128
    return pltpu.roll(tile, shift, 1) if shift else tile


def solve_kernel(
    sizes, s_ref, ov_ref, u_ref, halo_ref, uz_ref,
    m_ref, zs_ref, sx, sy, sxy, sz, p_ref, zp_ref, rx, ry, rz, r_ref, inv_ref, diag_ref,
    fx, fy, fxy, fz, s_send, s_recv, h_send, h_recv, f_send, f_recv,
):
    here = position(sizes)
    lower = [here[a] > 0 for a in range(3)]
    upper = [here[a] < sizes[a] - 1 for a in range(3)]
    steps = [(1, 0, 0), (0, 1, 0), (0, 0, 1), (1, 1, 0), (1, 0, 1), (0, 1, 1), (1, 1, 1)]

    def all_of(flags, step):
        wanted = [flags[a] for a in range(3) if step[a]]
        return functools.reduce(jnp.logical_and, wanted)

    def shifted(step, sign):
        return tuple(here[a] + sign * step[a] for a in range(3))

    barrier = pltpu.get_barrier_semaphore()
    known = jnp.int32(0)
    for step in steps:
        for flags, sign in ((lower, -1), (upper, 1)):
            present = all_of(flags, step)
            known = known + present.astype(jnp.int32)

            @pl.when(present)
            def _(step=step, sign=sign):
                pl.semaphore_signal(barrier, inc=1, device_id=shifted(step, sign), device_id_type=MESH)

    lane = lax.broadcasted_iota(jnp.int32, (8, 128), 1)
    sub = lax.broadcasted_iota(jnp.int32, (8, 128), 0)
    zero = jnp.zeros((8, 128), F32)

    for a, bufs in ((0, (sx, rx.at[:, 0])), (1, (sy, ry.at[:, 0])), (2, (sz.at[0], rz.at[:, 0]))):
        @pl.when(jnp.logical_not(lower[a]))
        def _(bufs=bufs):
            for buf in bufs:
                buf[...] = jnp.zeros(buf.shape, F32)
    for a, bufs in ((0, (fx, rx.at[:, 1])), (1, (fy, ry.at[:, 1])), (2, (fz.at[0], rz.at[:, 1]))):
        @pl.when(jnp.logical_not(upper[a]))
        def _(bufs=bufs):
            for buf in bufs:
                buf[...] = jnp.zeros(buf.shape, F32)
    for step, low_buf, high_buf in (
        (steps[3], sxy, fxy), (steps[4], sz.at[1], fz.at[1]),
        (steps[5], sz.at[2], fz.at[2]), (steps[6], sz.at[3], fz.at[3]),
    ):
        for flags, buf in ((lower, low_buf), (upper, high_buf)):
            @pl.when(jnp.logical_not(all_of(flags, step)))
            def _(buf=buf):
                buf[...] = jnp.zeros(buf.shape, F32)

    for part, tiles in ((0, 32), (1, 5)):
        packed = zero
        for i in range(tiles):
            tile = ov_ref[pl.ds(256 * part + 8 * i, 8), :]
            here_lanes = jnp.logical_and(lane >= 4 * i, lane < 4 * i + 4)
            packed = jnp.where(here_lanes, roll_to(tile, 0, 4 * i), packed)
        zs_ref[part] = packed
    for c in range(4):
        m_ref[c] = s_ref[0:256, 128 * c : 128 * c + 128].reshape(16, 2, 8, 128)
    pl.semaphore_wait(barrier, known)

    def corner_copies(sources, targets, send, recv, sign):
        copies = []
        for i, step in enumerate(steps):
            copies.append(pltpu.make_async_remote_copy(
                src_ref=sources[i], dst_ref=targets[i], send_sem=send.at[i], recv_sem=recv.at[i],
                device_id=shifted(step, sign), device_id_type=MESH,
            ))
        return copies

    def each(copies, flags, action):
        for copy, step in zip(copies, steps):
            @pl.when(all_of(flags, step))
            def _(copy=copy):
                action(copy)

    mass = corner_copies(
        [s_ref.at[256:272], s_ref.at[272:288], zs_ref.at[0], s_ref.at[288:289], zs_ref.at[1], zs_ref.at[1], zs_ref.at[1]],
        [sx, sy, sz.at[0], sxy, sz.at[1], sz.at[2], sz.at[3]], s_send, s_recv, 1,
    )
    each(mass, upper, lambda copy: copy.start())
    each(mass, lower, lambda copy: copy.wait_recv())

    for c in range(4):
        columns = slice(128 * c, 128 * c + 128)
        m_ref[c, 0] += sx[:, columns].reshape(2, 8, 128)
        from_y = sy[:, columns]
        near_z = [roll_to(sz[2], 8 + 4 * t + c, 0) for t in range(2)]
        for x in range(16):
            row = from_y[x : x + 1, :] + jnp.where(lane[0:1] == 0, near_z[x // 8][x % 8 : x % 8 + 1, :], 0.0)
            m_ref[c, x, 0, 0:1, :] += row
        for i in range(32):
            m_ref[c, i // 2, i % 2] += jnp.where(lane == 0, roll_to(sz[0], 4 * i + c, 0), 0.0)
        for t in range(2):
            m_ref[c, 0, t] += jnp.where(lane == 0, roll_to(sz[1], 4 * t + c, 0), 0.0)
        corner = sxy[:, columns] + jnp.where(lane[0:1] == 0, roll_to(sz[3], 16 + c, 0)[0:1], 0.0)
        m_ref[c, 0, 0, 0:1, :] += corner
    each(mass, upper, lambda copy: copy.wait_send())

    def pack(read, source):
        packed = zero
        for i in range(32):
            packed = jnp.where(lane == i, roll_to(read(i), source, i), packed)
        return packed

    def unpack(packed, target):
        mine = lane == target
        tiles = [jnp.where(mine, roll_to(packed, i, target), 0.0) for i in range(32)]
        return jnp.stack(tiles).reshape(16, 2, 8, 128)

    def face_copies(e, xs, ys):
        sources = [xs.at[15], xs.at[0], ys.at[:, 1, 7, :], ys.at[:, 0, 0, :], zp_ref.at[e, 1], zp_ref.at[e, 0]]
        targets = [rx.at[e, 0], rx.at[e, 1], ry.at[e, 0, :, 0, :], ry.at[e, 1, :, 0, :], rz.at[e, 0], rz.at[e, 1]]
        copies = []
        for d in range(6):
            step = tuple(int(a == d // 2) for a in range(3))
            copies.append(pltpu.make_async_remote_copy(
                src_ref=sources[d], dst_ref=targets[d], send_sem=h_send.at[e, d], recv_sem=h_recv.at[e, d],
                device_id=shifted(step, 1 - 2 * (d % 2)), device_id_type=MESH,
            ))
        return copies

    def arriving(d):
        return (lower, upper)[d % 2][d // 2]

    def leaving(d):
        return (upper, lower)[d % 2][d // 2]

    def each_face(copies, when, action):
        for d, copy in enumerate(copies):
            @pl.when(when(d))
            def _(copy=copy):
                action(copy)

    lanes4 = lax.broadcasted_iota(jnp.int32, (16, 2, 8, 128), 3)
    subs3 = lax.broadcasted_iota(jnp.int32, (16, 8, 128), 1)

    def x_sides(value, e):
        low = jnp.concatenate([rx[e, 0][None], value[:-1]], axis=0)
        high = jnp.concatenate([value[1:], rx[e, 1][None]], axis=0)
        return low, high

    def y_sides(value, e):
        down = pltpu.roll(value.reshape(32, 8, 128), 1, 1).reshape(16, 2, 8, 128)
        up = pltpu.roll(value.reshape(32, 8, 128), 7, 1).reshape(16, 2, 8, 128)
        first = subs3 == 0
        low = jnp.stack([jnp.where(first, ry[e, 0], down[:, 0]), jnp.where(first, down[:, 0], down[:, 1])], axis=1)
        last = subs3 == 7
        high = jnp.stack([jnp.where(last, up[:, 1], up[:, 0]), jnp.where(last, ry[e, 1], up[:, 1])], axis=1)
        return low, high

    def z_sides(value, e):
        flat = value.reshape(256, 128)
        down = pltpu.roll(flat, 1, 1).reshape(16, 2, 8, 128)
        up = pltpu.roll(flat, 127, 1).reshape(16, 2, 8, 128)
        low = jnp.where(lanes4 == 0, unpack(rz[e, 0], 0), down)
        high = jnp.where(lanes4 == 127, unpack(rz[e, 1], 127), up)
        return low, high

    def pack_faces(e, read):
        zp_ref[e, 0] = pack(read, 0)
        zp_ref[e, 1] = pack(read, 127)

    pack_faces(0, lambda i: m_ref[2, i // 2, i % 2])
    copies = face_copies(0, m_ref.at[0], m_ref.at[1])
    each_face(copies, leaving, lambda copy: copy.start())
    diagonal = 6.0 + base_screen + point_screen * m_ref[3]
    diag_ref[...] = diagonal
    inv_ref[...] = 1.0 / diagonal
    each_face(copies, arriving, lambda copy: copy.wait_recv())
    low, high = x_sides(m_ref[0], 0)
    total = high - low
    low, high = y_sides(m_ref[1], 0)
    total = total + (high - low)
    low, high = z_sides(m_ref[2], 0)
    total = -0.5 * (total + (high - low))
    r_ref[...] = total
    p_ref[1] = total * inv_ref[...]
    each_face(copies, leaving, lambda copy: copy.wait_send())

    for k, (keep, push) in enumerate(sweep_factors(), 1):
        pack_faces(k, lambda i: p_ref[k, i // 2, i % 2])
        copies = face_copies(k, p_ref.at[k], p_ref.at[k])
        each_face(copies, leaving, lambda copy: copy.start())
        p = p_ref[k]
        if k == 1:
            u_ref[...] = p
        else:
            u_ref[...] += p
        each_face(copies, arriving, lambda copy: copy.wait_recv())
        around = sum(x_sides(p, k)) + sum(y_sides(p, k)) + sum(z_sides(p, k))
        r = r_ref[...] - (diag_ref[...] * p - around)
        r_ref[...] = r
        following = keep * p + push * (r * inv_ref[...])
        if k < ITERS - 1:
            p_ref[k + 1] = following
        else:
            u_ref[...] += following
        each_face(copies, leaving, lambda copy: copy.wait_send())

    zp_ref[6, 0] = pack(lambda i: u_ref[i // 2, i % 2], 0)
    layer = corner_copies(
        [u_ref.at[0], u_ref.at[:, 0, 0, :], zp_ref.at[6, 0], u_ref.at[0, 0, 0:1], zp_ref.at[6, 0], zp_ref.at[6, 0], zp_ref.at[6, 0]],
        [fx, fy, fz.at[0], fxy, fz.at[1], fz.at[2], fz.at[3]], f_send, f_recv, -1,
    )
    each(layer, lower, lambda copy: copy.start())
    each(layer, upper, lambda copy: copy.wait_recv())
    halo_ref[0:16] = fx[...].reshape(16, 128)
    halo_ref[16:32] = fy[...]
    halo_ref[32:40] = jnp.where(sub == 0, jnp.broadcast_to(fxy[...], (8, 128)), 0.0)
    halo_ref[40:48] = zero
    for i in range(32):
        uz_ref[8 * i : 8 * i + 8] = roll_to(fz[0], i, 0)
    for t in range(2):
        uz_ref[256 + 8 * t : 264 + 8 * t] = roll_to(fz[1], t, 0)
        picked = jnp.where(lane == 2 * (8 * t + sub), jnp.broadcast_to(fz[2, 0:1], (8, 128)), 0.0)
        column = jnp.sum(picked, axis=1, keepdims=True)
        uz_ref[272 + 8 * t : 280 + 8 * t] = jnp.broadcast_to(column, (8, 128))
    uz_ref[288:296] = jnp.where(sub == 0, fz[3], 0.0)
    uz_ref[296:304] = zero
    each(layer, lower, lambda copy: copy.wait_send())


def params(collective_id=None, limit=None):
    extra = {} if collective_id is None else {"collective_id": collective_id, "has_side_effects": True}
    return pltpu.CompilerParams(vmem_limit_bytes=limit or 48 * 1024 * 1024, **extra)


def on_device(sizes, point_data, point_cells, send_counts):
    data = jnp.transpose(point_data[0], (1, 2, 0))
    cells = jnp.transpose(point_cells[0], (1, 2, 0))
    dma = pltpu.SemaphoreType.DMA
    points = pl.pallas_call(
        functools.partial(route_kernel, sizes),
        out_shape=jax.ShapeDtypeStruct((CHANNELS, CAP, DEVICES), F32),
        in_specs=[vmem()] * 3,
        out_specs=vmem(),
        scratch_shapes=[pltpu.VMEM((DEVICES, WIDTH), F32)] * 2 + [pltpu.VMEM((1, WIDTH), F32), dma, dma],
        compiler_params=params(0),
        name="route",
    )(data, cells, send_counts)
    mass, over = pl.pallas_call(
        splat_kernel,
        out_shape=[jax.ShapeDtypeStruct((ROWS, 512), F32), jax.ShapeDtypeStruct((ROWS, 128), F32)],
        in_specs=[vmem()],
        out_specs=[vmem()] * 2,
        scratch_shapes=[pltpu.VMEM((ROWS, 3 * POINTS), BF16), pltpu.VMEM((528, 3 * POINTS), BF16)],
        compiler_params=params(),
        name="splat",
    )(points)
    field = (16, 2, 8, 128)
    shapes = [
        (4, *field), (2, 8, 128), (16, 512), (16, 512), (1, 512), (4, 8, 128),
        (6, *field), (7, 2, 8, 128), (6, 2, 2, 8, 128), (6, 2, 16, 1, 128), (6, 2, 8, 128), field, field, field,
        (2, 8, 128), (16, 128), (1, 128), (4, 8, 128),
    ]
    u, halo, uz = pl.pallas_call(
        functools.partial(solve_kernel, sizes),
        out_shape=[jax.ShapeDtypeStruct(s, F32) for s in (field, (48, 128), (ROWS, 128))],
        in_specs=[vmem()] * 2,
        out_specs=[vmem()] * 3,
        scratch_shapes=[pltpu.VMEM(s, F32) for s in shapes]
        + [dma((7,)), dma((7,)), dma((6, 6)), dma((6, 6)), dma((7,)), dma((7,))],
        compiler_params=params(1),
        name="solve",
    )(mass, over)
    values = pl.pallas_call(
        interp_kernel,
        out_shape=jax.ShapeDtypeStruct((CAP, DEVICES), F32),
        in_specs=[vmem()] * 4,
        out_specs=vmem(),
        scratch_shapes=[pltpu.VMEM((ROWS, 512), BF16), pltpu.VMEM((512, POINTS), BF16)],
        compiler_params=params(),
        name="interp",
    )(points, u.reshape(256, 128), halo, uz)
    returned = pl.pallas_call(
        functools.partial(return_kernel, sizes),
        out_shape=jax.ShapeDtypeStruct((CAP, DEVICES), F32),
        in_specs=[vmem()] * 2,
        out_specs=vmem(),
        scratch_shapes=[pltpu.VMEM((DEVICES, DEVICES), F32)] * 2 + [pltpu.VMEM((1, DEVICES), F32), dma, dma],
        compiler_params=params(2),
        name="give_back",
    )(values, send_counts)
    return u.reshape(16, 16, 128), returned.T[None]


def solution(mesh):
    sizes = tuple(mesh.shape[name] for name in ("gx", "gy", "gz"))
    spread_over = ("gx", "gy", "gz")
    in_specs = (P(spread_over, None, None, None), P(spread_over, None, None, None), P(spread_over, None))
    out_specs = (P("gx", "gy", "gz"), P(spread_over, None, None))
    return jax.shard_map(
        functools.partial(on_device, sizes), mesh=mesh, in_specs=in_specs, out_specs=out_specs, check_vma=False
    )
```

time: 750 us -> 75.4 us (0.10); the launches traced: 740 us -> 75.2 us
  other arithmetic: 273 us -> 0 us
  local copies, waits for them, and re-layouts: 226 us -> 3.61 us
  starting transfers between devices: 132 us -> 0 us
  waiting for transfers between devices: 94.1 us -> 0 us
  Pallas kernels: 0 us -> 70.9 us
  blocking collectives: 12.4 us -> 0 us
    scatter-add x9 -> x0, other arithmetic: 264 us -> none  [the longest x8 264 us: on_device(): volume = volume.at[:, linear_at.reshape(-1)].add(contrib)]
    gather x16 -> x0, local copies, waits for them, and re-layouts: 185 us -> none  [on_device(): extended[linear_at]]
    ppermute x45 -> x0, starting transfers between devices: 116 us -> none  [the longest x21 76.4 us: with_halo(): lax.ppermute(lax.slice_in_dim(block, block.shape[dim] - width, None, axis...]
    ppermute x45 -> x0, waiting for transfers between devices: 79.3 us -> none  [the longest x21 58.3 us: with_halo(): lax.ppermute(lax.slice_in_dim(block, 0, width, axis=dim), axis, backward)]
    pallas_call x0 -> x5, Pallas kernels: none -> 70.9 us  [the longest x1 28.9 us: on_device(): pl.pallas_call(functools.partial(solve_kernel, sizes), out_shape=[jax.Sha...]
    all_to_all x2 -> x0, starting transfers between devices: 15.4 us -> none  [the longest x1 11.5 us: on_device(): lax.all_to_all(point_cells, ('gx', 'gy', 'gz'), split_axis=1, concat_axis...]
    another operation x10 -> x0, local copies, waits for them, and re-layouts: 15.3 us -> none  [the longest x8 14.6 us: on_device(): jnp.stack([got_data[:, 0, :] * point_mass, got_data[:, 1, :] * point_mass...]
    all_to_all x2 -> x0, waiting for transfers between devices: 14.9 us -> none  [the longest x1 8.94 us: on_device(): lax.all_to_all(outgoing, ('gx', 'gy', 'gz'), split_axis=1, concat_axis=0,...]
  transfers between devices with their start and end apart: 47 -> 0, of which waited for: 32 -> 0; matrix products, arithmetic and copies ran while one was open for 1% -> 0% of each run, Pallas kernels for 0% -> 0%
where the time goes in v1:
time: 75.4 us; the launch traced here: 75.2 us
  Pallas kernels  70.9 us (94%)
  local copies, waits for them, and re-layouts  3.61 us (5%)
    pallas_call x1, Pallas kernels, on_device(): pl.pallas_call(functools.partial(solve_kernel, sizes), out_shape=[jax.Sha...  28.9 us
    pallas_call x1, Pallas kernels, on_device(): pl.pallas_call(functools.partial(route_kernel, sizes), out_shape=jax.Shap...  18 us
    pallas_call x1, Pallas kernels, on_device(): pl.pallas_call(functools.partial(return_kernel, sizes), out_shape=jax.Sha...  13.5 us
    pallas_call x1, Pallas kernels, on_device(): pl.pallas_call(splat_kernel, out_shape=[jax.ShapeDtypeStruct((ROWS, 512),...  7.59 us
    unnamed x8, local copies, waits for them, and re-layouts  3.61 us
    pallas_call x1, Pallas kernels, on_device(): pl.pallas_call(interp_kernel, out_shape=jax.ShapeDtypeStruct((CAP, DEVICE...  3.02 us

profile of v1, /device:TPU:1, one launch (start us, length us, event | category | flops | bytes accessed | tf_op | source)
XLA Modules:
  0.0 75.2 jit_solution(10638726953831222066)
XLA Ops:
  0.6 0.0 copy-start.2
  0.6 0.6 copy-done.2
  1.3 0.0 copy-start
  1.3 0.9 %copy-done = f32[1,128,7,32]{1,3,2,0:T(8,128)S(1)} copy-done((f32[1,128,7,32]{1,3,2,0:T(8,128)S(1)}, f32[1,128,7,32]{1,3,2,0:T(8,128)}, u32[]{:S(2)}) %copy-start) | copy-done | bytes 114712
  2.2 0.0 copy-start.1
  2.2 0.8 %copy-done.1 = s32[1,128,3,32]{1,3,2,0:T(8,128)S(1)} copy-done((s32[1,128,3,32]{1,3,2,0:T(8,128)S(1)}, s32[1,128,3,32]{1,3,2,0:T(8,128)}, u32[]{:S(2)}) %copy-start.1) | copy-done | bytes 49176
  3.0 18.0 %route.1.d_ref = f32[10,32,128]{2,1,0:T(8,128)S(1)} custom-call(f32[7,32,128]{2,1,0:T(8,128)S(1)} %bitcast.13, s32[3,32,128]{2,1,0:T(8,128)S(1)} %bitcast.15, s32[1,128]{1,0:T(1,128)S(1)} %copy-done.2), custom_call_target="tpu_custom_call" | custom-call | tf_op jit(solution)/shard_map/route/pallas_call | solution.py:474
  20.9 7.6 %splat.1 = (f32[304,512]{1,0:T(8,128)S(1)}, f32[304,128]{1,0:T(8,128)S(1)}) custom-call(f32[10,32,128]{2,1,0:T(8,128)S(1)} %route.1.d_ref), custom_call_target="tpu_custom_call" | custom-call | tf_op jit(solution)/shard_map/splat/pallas_call | solution.py:483
  28.5 28.9 %solve.1 = (f32[16,2,8,128]{3,2,1,0:T(8,128)S(1)}, f32[48,128]{1,0:T(8,128)S(1)}, f32[304,128]{1,0:T(8,128)S(1)}) custom-call(f32[304,512]{1,0:T(8,128)S(1)} %get-tuple-element.7.s_ref, f32[304,128]{1,0:T(8,128)S(1)} %get-tuple-element.8.ov_ref), custom_call_target="tpu_custom_call" | custom-call | tf_op jit(solution)/shard_map/solve/pallas_call | solution.py:498
  57.4 3.0 %interp.1.values_ref = f32[32,128]{1,0:T(8,128)S(1)} custom-call(f32[10,32,128]{2,1,0:T(8,128)S(1)} %route.1.d_ref, f32[256,128]{1,0:T(8,128)S(1)} %bitcast.11, f32[48,128]{1,0:T(8,128)S(1)} %get-tuple-element.10.halo_ref, f32[304,128]{1,0:T(8,128)S(1)} %get-tuple-element.11.uz_ref), custom_call_target="tpu_custom_call" | custom-call | tf_op jit(solution)/shard_map/interp/pallas_call | solution.py:508
  60.4 13.5 %give_back.1 = f32[32,128]{1,0:T(8,128)S(1)} custom-call(f32[32,128]{1,0:T(8,128)S(1)} %interp.1.values_ref, s32[1,128]{1,0:T(1,128)S(1)} %copy-done.2), custom_call_target="tpu_custom_call" | custom-call | tf_op jit(solution)/shard_map/give_back/pallas_call | solution.py:517
  73.9 0.7 copy.7
  74.6 0.6 copy.8
Async XLA Ops:
  0.6 0.7 copy-start.2
  1.3 0.9 %copy-start = (f32[1,128,7,32]{1,3,2,0:T(8,128)S(1)}, f32[1,128,7,32]{1,3,2,0:T(8,128)}, u32[]{:S(2)}) copy-start(f32[1,128,7,32]{1,3,2,0:T(8,128)} %param.3) | copy-start | bytes 344068
  2.2 0.8 %copy-start.1 = (s32[1,128,3,32]{1,3,2,0:T(8,128)S(1)}, s32[1,128,3,32]{1,3,2,0:T(8,128)}, u32[]{:S(2)}) copy-start(s32[1,128,3,32]{1,3,2,0:T(8,128)} %param.4) | copy-start | bytes 147460

commit v2 on v1

--- a/solution.py
+++ b/solution.py
@@ -47,59 +47,54 @@
     return pl.BlockSpec(memory_space=pltpu.VMEM)
 
 
-def greet_all(sizes, me):
+def greet(sizes, here, relay_y, relay_x):
     barrier = pltpu.get_barrier_semaphore()
 
-    @pl.loop(1, DEVICES)
-    def _(step):
-        other = lax.rem(me + step, DEVICES)
-        pl.semaphore_signal(barrier, inc=1, device_id=coordinates(sizes, other), device_id_type=MESH)
-
-
-def exchange_rows(sizes, me, send, recv, sent, send_sem, recv_sem):
-    pl.semaphore_wait(pltpu.get_barrier_semaphore(), DEVICES - 1)
-
-    @pl.loop(1, DEVICES)
-    def _(step):
-        other = lax.rem(me + step, DEVICES)
+    def tell(axis, semaphore):
+        for step in range(1, sizes[axis]):
+            target = tuple(lax.rem(here[a] + step, sizes[a]) if a == axis else here[a] for a in range(3))
+            pl.semaphore_signal(semaphore, inc=1, device_id=target, device_id_type=MESH)
+
+    for axis in range(3):
+        tell(axis, barrier)
+    pl.semaphore_wait(barrier, sum(sizes) - 3)
+    tell(1, relay_y)
+    pl.semaphore_wait(relay_y, sizes[1] - 1)
+    tell(0, relay_x)
+    pl.semaphore_wait(relay_x, sizes[0] - 1)
+
+
+def exchange_rows(me, send, recv, sent, send_sem, recv_sem):
+    def post(step):
+        other = me ^ ((step * 37) & (DEVICES - 1))
         pltpu.make_async_remote_copy(
             src_ref=send.at[pl.ds(other, 1)],
             dst_ref=recv.at[pl.ds(me, 1)],
             send_sem=send_sem,
             recv_sem=recv_sem,
-            device_id=coordinates(sizes, other),
-            device_id_type=MESH,
+            device_id=other,
+            device_id_type=pl.DeviceIdType.LOGICAL,
         ).start()
 
+    @pl.loop(0, DEVICES - 8, step=8)
+    def _(step):
+        for q in range(8):
+            post(step + q + 1)
+
+    for q in range(DEVICES - 7, DEVICES):
+        post(q)
     pltpu.make_async_copy(send.at[pl.ds(me, 1)], recv.at[pl.ds(me, 1)], recv_sem).start()
     pltpu.make_async_copy(send.at[pl.ds(me, 1)], sent, send_sem).start()
-    pltpu.make_async_copy(send, recv, send_sem).wait()
     pltpu.make_async_copy(send, recv, recv_sem).wait()
 
 
-def route_kernel(sizes, data_ref, cells_ref, counts_ref, out_ref, send, recv, sent, send_sem, recv_sem):
-    gx, gy, gz = position(sizes)
-    me = (gx * sizes[1] + gy) * sizes[2] + gz
-    greet_all(sizes, me)
+def prepare_rows(data_ref, cells_ref, counts_ref, send):
     slot = lax.broadcasted_iota(jnp.int32, (CAP, DEVICES), 0)
     weight = jnp.where(slot < counts_ref[...], data_ref[3], 0.0)
     parts = [data_ref[c] * weight for c in range(3)] + [weight]
     parts += [data_ref[4 + c] for c in range(3)] + [cells_ref[c].astype(F32) for c in range(3)]
     parts += [jnp.zeros((WIDTH - CAP * CHANNELS, DEVICES), F32)]
     send[...] = jnp.concatenate(parts, axis=0).T
-    exchange_rows(sizes, me, send, recv, sent, send_sem, recv_sem)
-    out_ref[...] = recv[...].T[: CAP * CHANNELS].reshape(CHANNELS, CAP, DEVICES)
-
-
-def return_kernel(sizes, values_ref, counts_ref, out_ref, send, recv, sent, send_sem, recv_sem):
-    gx, gy, gz = position(sizes)
-    me = (gx * sizes[1] + gy) * sizes[2] + gz
-    greet_all(sizes, me)
-    padded = jnp.concatenate([values_ref[...], jnp.zeros((DEVICES - CAP, DEVICES), F32)], axis=0)
-    send[...] = padded.T
-    exchange_rows(sizes, me, send, recv, sent, send_sem, recv_sem)
-    slot = lax.broadcasted_iota(jnp.int32, (CAP, DEVICES), 0)
-    out_ref[...] = jnp.where(slot < counts_ref[...], recv[...].T[:CAP], 0.0)
 
 
 def split(value):
@@ -122,9 +117,7 @@
     return split(wide)
 
 
-def splat_kernel(d_ref, acc_ref, ov_ref, a_ref, b_ref):
-    acc_ref[...] = jnp.zeros_like(acc_ref)
-    ov_ref[...] = jnp.zeros_like(ov_ref)
+def build_tiles(d_ref, group, a_ref, b_ref):
     iota = lax.broadcasted_iota(jnp.int32, (16, POINTS), 0).astype(F32).astype(BF16)
     zero = jnp.zeros((16, POINTS), BF16)
 
@@ -140,51 +133,69 @@
         b_ref[rows, POINTS : 2 * POINTS] = high
         b_ref[rows, 2 * POINTS : 3 * POINTS] = low
 
-    @pl.loop(0, CAP * DEVICES // POINTS)
-    def _(group):
-        v = [point_rows(d_ref, group, c) for c in range(4)]
-        fx, fy, fz, cx, cy, cz = [point_rows(d_ref, group, 4 + c) for c in range(6)]
-        bx, by, bz = spread(cx), spread(cy), spread(cz)
-        y0, y1 = by == iota, (by + 1.0).astype(BF16) == iota
-        near = [], []
-        for along, out in ((1.0 - fx, 0), (fx, 1)):
-            w0 = spread_split(along * (1.0 - fy))
-            w1 = spread_split(along * fy)
-            for part in range(2):
-                near[out].append(jnp.where(y0, w0[part], jnp.where(y1, w1[part], zero)))
-        for x in range(17):
-            x0, x1 = bx == x, bx == x - 1
-            high, low = [jnp.where(x0, near[0][part], jnp.where(x1, near[1][part], zero)) for part in range(2)]
-            store_a(16 * x, high, low)
-        edge = jnp.where(cy == 15.0, fy, 0.0)
-        e0, e1 = spread_split((1.0 - fx) * edge), spread_split(fx * edge)
-        for t in range(2):
-            at = iota + jnp.asarray(16 * t, BF16)
-            x0, x1 = bx == at, (bx + 1.0).astype(BF16) == at
-            high, low = [jnp.where(x0, e0[part], jnp.where(x1, e1[part], zero)) for part in range(2)]
-            store_a(272 + 16 * t, high, low)
-        g0 = [spread_split(v[c] * (1.0 - fz)) for c in range(4)]
-        g1 = [spread_split(v[c] * fz) for c in range(4)]
-        for t in range(8):
-            at = iota + jnp.asarray(16 * t, BF16)
-            z0, z1 = bz == at, (bz + 1.0).astype(BF16) == at
-            for c in range(4):
-                high, low = [jnp.where(z0, g0[c][part], jnp.where(z1, g1[c][part], zero)) for part in range(2)]
-                store_b(128 * c + 16 * t, high, low)
-        top = bz == 127
-        high, low = zero, zero
+    v = [point_rows(d_ref, group, c) for c in range(4)]
+    fx, fy, fz, cx, cy, cz = [point_rows(d_ref, group, 4 + c) for c in range(6)]
+    bx, by, bz = spread(cx), spread(cy), spread(cz)
+    y0, y1 = by == iota, (by + 1.0).astype(BF16) == iota
+    near = [], []
+    for along, out in ((1.0 - fx, 0), (fx, 1)):
+        w0 = spread_split(along * (1.0 - fy))
+        w1 = spread_split(along * fy)
+        for part in range(2):
+            near[out].append(jnp.where(y0, w0[part], jnp.where(y1, w1[part], zero)))
+    for x in range(17):
+        x0, x1 = bx == x, bx == x - 1
+        high, low = [jnp.where(x0, near[0][part], jnp.where(x1, near[1][part], zero)) for part in range(2)]
+        store_a(16 * x, high, low)
+    edge = jnp.where(cy == 15.0, fy, 0.0)
+    e0, e1 = spread_split((1.0 - fx) * edge), spread_split(fx * edge)
+    for t in range(2):
+        at = iota + jnp.asarray(16 * t, BF16)
+        x0, x1 = bx == at, (bx + 1.0).astype(BF16) == at
+        high, low = [jnp.where(x0, e0[part], jnp.where(x1, e1[part], zero)) for part in range(2)]
+        store_a(272 + 16 * t, high, low)
+    g0 = [spread_split(v[c] * (1.0 - fz)) for c in range(4)]
+    g1 = [spread_split(v[c] * fz) for c in range(4)]
+    for t in range(8):
+        at = iota + jnp.asarray(16 * t, BF16)
+        z0, z1 = bz == at, (bz + 1.0).astype(BF16) == at
         for c in range(4):
-            here = jnp.logical_and(top, iota == c)
-            high, low = jnp.where(here, g1[c][0], high), jnp.where(here, g1[c][1], low)
-        store_b(512, high, low)
-        dims = (((1,), (1,)), ((), ()))
-        acc_ref[...] += lax.dot_general(a_ref[...], b_ref[0:512, :], dims, preferred_element_type=F32)
-        ov_ref[:, 0:16] += lax.dot_general(a_ref[...], b_ref[512:528, :], dims, preferred_element_type=F32)
-
-
-def interp_kernel(d_ref, u_ref, halo_ref, uz_ref, out_ref, l_ref, r_ref):
-    for first, source in ((0, u_ref), (256, halo_ref)):
-        value = source[...]
+            high, low = [jnp.where(z0, g0[c][part], jnp.where(z1, g1[c][part], zero)) for part in range(2)]
+            store_b(128 * c + 16 * t, high, low)
+    top = bz == 127
+    high, both = zero, zero
+    for c in range(4):
+        here = jnp.logical_and(top, iota == c)
+        high = jnp.where(here, g1[c][0], high)
+        both = jnp.where(jnp.logical_and(top, iota == c + 4), g1[c][1], both)
+    b_ref[512:528, 0:POINTS] = jnp.where(iota < 4, high, both)
+    b_ref[512:528, POINTS : 2 * POINTS] = high
+
+
+def multiply_tiles(a_ref, b_ref, acc_ref, ov_ref):
+    dims = (((1,), (1,)), ((), ()))
+    acc_ref[...] += lax.dot_general(a_ref[...], b_ref[0:512, :], dims, preferred_element_type=F32)
+    ov_ref[:, 0:16] += lax.dot_general(
+        a_ref[:, 0 : 2 * POINTS], b_ref[512:528, 0 : 2 * POINTS], dims, preferred_element_type=F32
+    )
+
+
+def splat_points(d_ref, acc_ref, ov_ref, a0, b0, a1, b1):
+    acc_ref[...] = jnp.zeros_like(acc_ref)
+    ov_ref[...] = jnp.zeros_like(ov_ref)
+    groups = CAP * DEVICES // POINTS
+    build_tiles(d_ref, 0, a0, b0)
+
+    @pl.loop(0, groups // 2)
+    def _(pair):
+        build_tiles(d_ref, 2 * pair + 1, a1, b1)
+        multiply_tiles(a0, b0, acc_ref, ov_ref)
+        build_tiles(d_ref, jnp.minimum(2 * pair + 2, groups - 1), a0, b0)
+        multiply_tiles(a1, b1, acc_ref, ov_ref)
+
+
+def interpolate(d_ref, u_ref, halo_ref, uz_ref, out_ref, l_ref, r_ref):
+    for first, value in ((0, u_ref[...].reshape(256, 128)), (256, halo_ref[...])):
         rows = pl.ds(first, value.shape[0])
         high, low = split(value)
         l_ref[rows, 0:128] = high
@@ -238,12 +249,11 @@
     return pltpu.roll(tile, shift, 1) if shift else tile
 
 
-def solve_kernel(
-    sizes, s_ref, ov_ref, u_ref, halo_ref, uz_ref,
+def solve(
+    sizes, here, s_ref, ov_ref, u_ref, halo_ref, uz_ref,
     m_ref, zs_ref, sx, sy, sxy, sz, p_ref, zp_ref, rx, ry, rz, r_ref, inv_ref, diag_ref,
     fx, fy, fxy, fz, s_send, s_recv, h_send, h_recv, f_send, f_recv,
 ):
-    here = position(sizes)
     lower = [here[a] > 0 for a in range(3)]
     upper = [here[a] < sizes[a] - 1 for a in range(3)]
     steps = [(1, 0, 0), (0, 1, 0), (0, 0, 1), (1, 1, 0), (1, 0, 1), (0, 1, 1), (1, 1, 1)]
@@ -254,17 +264,6 @@
 
     def shifted(step, sign):
         return tuple(here[a] + sign * step[a] for a in range(3))
-
-    barrier = pltpu.get_barrier_semaphore()
-    known = jnp.int32(0)
-    for step in steps:
-        for flags, sign in ((lower, -1), (upper, 1)):
-            present = all_of(flags, step)
-            known = known + present.astype(jnp.int32)
-
-            @pl.when(present)
-            def _(step=step, sign=sign):
-                pl.semaphore_signal(barrier, inc=1, device_id=shifted(step, sign), device_id_type=MESH)
 
     lane = lax.broadcasted_iota(jnp.int32, (8, 128), 1)
     sub = lax.broadcasted_iota(jnp.int32, (8, 128), 0)
@@ -293,12 +292,12 @@
         packed = zero
         for i in range(tiles):
             tile = ov_ref[pl.ds(256 * part + 8 * i, 8), :]
+            tile = tile + pltpu.roll(tile, 124, 1)
             here_lanes = jnp.logical_and(lane >= 4 * i, lane < 4 * i + 4)
             packed = jnp.where(here_lanes, roll_to(tile, 0, 4 * i), packed)
         zs_ref[part] = packed
     for c in range(4):
         m_ref[c] = s_ref[0:256, 128 * c : 128 * c + 128].reshape(16, 2, 8, 128)
-    pl.semaphore_wait(barrier, known)
 
     def corner_copies(sources, targets, send, recv, sign):
         copies = []
@@ -462,67 +461,68 @@
     each(layer, lower, lambda copy: copy.wait_send())
 
 
-def params(collective_id=None, limit=None):
-    extra = {} if collective_id is None else {"collective_id": collective_id, "has_side_effects": True}
-    return pltpu.CompilerParams(vmem_limit_bytes=limit or 48 * 1024 * 1024, **extra)
+def kernel(sizes, data_hbm, cells_hbm, counts_hbm, u_ref, out_ref, *scratch):
+    (data_ref, cells_ref, counts_ref, send, recv, sent, d_ref, a0, b0, a1, b1, acc_ref, ov_ref,
+     l_ref, r_ref, halo_ref, uz_ref, val_ref, back_send, back_recv, back_sent,
+     in_sem, send_sem, recv_sem, relay_y, relay_x, *rest) = scratch
+    here = position(sizes)
+    me = (here[0] * sizes[1] + here[1]) * sizes[2] + here[2]
+    loads = [
+        pltpu.make_async_copy(source, target, in_sem.at[i])
+        for i, (source, target) in enumerate(((data_hbm, data_ref), (cells_hbm, cells_ref), (counts_hbm, counts_ref)))
+    ]
+    for load in loads:
+        load.start()
+    for load in loads:
+        load.wait()
+    prepare_rows(data_ref, cells_ref, counts_ref, send)
+    greet(sizes, here, relay_y, relay_x)
+    exchange_rows(me, send, recv, sent, send_sem.at[0], recv_sem.at[0])
+    d_ref[...] = recv[...].T[: CAP * CHANNELS].reshape(CHANNELS, CAP, DEVICES)
+    splat_points(d_ref, acc_ref, ov_ref, a0, b0, a1, b1)
+    solve(sizes, here, acc_ref, ov_ref, u_ref, halo_ref, uz_ref, *rest)
+    interpolate(d_ref, u_ref, halo_ref, uz_ref, val_ref, l_ref, r_ref)
+    padded = jnp.concatenate([val_ref[...], jnp.zeros((DEVICES - CAP, DEVICES), F32)], axis=0)
+    back_send[...] = padded.T
+    exchange_rows(me, back_send, back_recv, back_sent, send_sem.at[1], recv_sem.at[1])
+    slot = lax.broadcasted_iota(jnp.int32, (CAP, DEVICES), 0)
+    out_ref[...] = jnp.where(slot < counts_ref[...], back_recv[...].T[:CAP], 0.0)
+    pltpu.make_async_copy(send, recv, send_sem.at[0]).wait()
+    pltpu.make_async_copy(back_send, back_recv, send_sem.at[1]).wait()
 
 
 def on_device(sizes, point_data, point_cells, send_counts):
     data = jnp.transpose(point_data[0], (1, 2, 0))
     cells = jnp.transpose(point_cells[0], (1, 2, 0))
-    dma = pltpu.SemaphoreType.DMA
-    points = pl.pallas_call(
-        functools.partial(route_kernel, sizes),
-        out_shape=jax.ShapeDtypeStruct((CHANNELS, CAP, DEVICES), F32),
-        in_specs=[vmem()] * 3,
-        out_specs=vmem(),
-        scratch_shapes=[pltpu.VMEM((DEVICES, WIDTH), F32)] * 2 + [pltpu.VMEM((1, WIDTH), F32), dma, dma],
-        compiler_params=params(0),
-        name="route",
-    )(data, cells, send_counts)
-    mass, over = pl.pallas_call(
-        splat_kernel,
-        out_shape=[jax.ShapeDtypeStruct((ROWS, 512), F32), jax.ShapeDtypeStruct((ROWS, 128), F32)],
-        in_specs=[vmem()],
-        out_specs=[vmem()] * 2,
-        scratch_shapes=[pltpu.VMEM((ROWS, 3 * POINTS), BF16), pltpu.VMEM((528, 3 * POINTS), BF16)],
-        compiler_params=params(),
-        name="splat",
-    )(points)
+    dma, regular = pltpu.SemaphoreType.DMA, pltpu.SemaphoreType.REGULAR
     field = (16, 2, 8, 128)
     shapes = [
+        ((7, CAP, DEVICES), F32), ((3, CAP, DEVICES), jnp.int32), ((1, DEVICES), jnp.int32),
+        ((DEVICES, WIDTH), F32), ((DEVICES, WIDTH), F32), ((1, WIDTH), F32), ((CHANNELS, CAP, DEVICES), F32),
+        ((ROWS, 3 * POINTS), BF16), ((528, 3 * POINTS), BF16), ((ROWS, 3 * POINTS), BF16), ((528, 3 * POINTS), BF16),
+        ((ROWS, 512), F32), ((ROWS, 128), F32), ((ROWS, 512), BF16), ((512, POINTS), BF16),
+        ((48, 128), F32), ((ROWS, 128), F32), ((CAP, DEVICES), F32),
+        ((DEVICES, DEVICES), F32), ((DEVICES, DEVICES), F32), ((1, DEVICES), F32),
+    ]
+    halo_shapes = [
         (4, *field), (2, 8, 128), (16, 512), (16, 512), (1, 512), (4, 8, 128),
         (6, *field), (7, 2, 8, 128), (6, 2, 2, 8, 128), (6, 2, 16, 1, 128), (6, 2, 8, 128), field, field, field,
         (2, 8, 128), (16, 128), (1, 128), (4, 8, 128),
     ]
-    u, halo, uz = pl.pallas_call(
-        functools.partial(solve_kernel, sizes),
-        out_shape=[jax.ShapeDtypeStruct(s, F32) for s in (field, (48, 128), (ROWS, 128))],
-        in_specs=[vmem()] * 2,
-        out_specs=[vmem()] * 3,
-        scratch_shapes=[pltpu.VMEM(s, F32) for s in shapes]
+    u, returned = pl.pallas_call(
+        functools.partial(kernel, sizes),
+        out_shape=[jax.ShapeDtypeStruct(s, F32) for s in (field, (CAP, DEVICES))],
+        in_specs=[pl.BlockSpec(memory_space=pl.ANY)] * 3,
+        out_specs=[vmem()] * 2,
+        scratch_shapes=[pltpu.VMEM(*s) for s in shapes]
+        + [dma((3,)), dma((2,)), dma((2,)), regular, regular]
+        + [pltpu.VMEM(s, F32) for s in halo_shapes]
         + [dma((7,)), dma((7,)), dma((6, 6)), dma((6, 6)), dma((7,)), dma((7,))],
-        compiler_params=params(1),
-        name="solve",
-    )(mass, over)
-    values = pl.pallas_call(
-        interp_kernel,
-        out_shape=jax.ShapeDtypeStruct((CAP, DEVICES), F32),
-        in_specs=[vmem()] * 4,
-        out_specs=vmem(),
-        scratch_shapes=[pltpu.VMEM((ROWS, 512), BF16), pltpu.VMEM((512, POINTS), BF16)],
-        compiler_params=params(),
-        name="interp",
-    )(points, u.reshape(256, 128), halo, uz)
-    returned = pl.pallas_call(
-        functools.partial(return_kernel, sizes),
-        out_shape=jax.ShapeDtypeStruct((CAP, DEVICES), F32),
-        in_specs=[vmem()] * 2,
-        out_specs=vmem(),
-        scratch_shapes=[pltpu.VMEM((DEVICES, DEVICES), F32)] * 2 + [pltpu.VMEM((1, DEVICES), F32), dma, dma],
-        compiler_params=params(2),
-        name="give_back",
-    )(values, send_counts)
+        compiler_params=pltpu.CompilerParams(
+            vmem_limit_bytes=24 * 1024 * 1024, collective_id=0, has_side_effects=True
+        ),
+        name="reconstruct",
+    )(data, cells, send_counts)
     return u.reshape(16, 16, 128), returned.T[None]
 
 

time: 75.4 us -> 65.8 us (0.87)
  Pallas kernels: 70.9 us -> 61.4 us
    pallas_call x5 -> x1, Pallas kernels: 70.9 us -> 61.4 us  [on_device(): pl.pallas_call(functools.partial(kernel, sizes), out_shape=[jax.ShapeDtyp...]
where the time goes in v2:
time: 65.8 us; the launch traced here: 65.7 us
  Pallas kernels  61.4 us (93%)
  local copies, waits for them, and re-layouts  3.61 us (5%)
    pallas_call x1, Pallas kernels, on_device(): pl.pallas_call(functools.partial(kernel, sizes), out_shape=[jax.ShapeDtyp...  61.4 us
    unnamed x8, local copies, waits for them, and re-layouts  3.61 us

profile of v2, /device:TPU:1, one launch (start us, length us, event | category | flops | bytes accessed | tf_op | source)
XLA Modules:
  0.0 65.7 jit_solution(4437111885647644271)
XLA Ops:
  0.6 0.0 copy-start.2
  0.6 0.6 copy-done.2
  1.3 0.0 copy-start
  1.3 0.9 %copy-done = f32[1,128,7,32]{1,3,2,0:T(8,128)S(1)} copy-done((f32[1,128,7,32]{1,3,2,0:T(8,128)S(1)}, f32[1,128,7,32]{1,3,2,0:T(8,128)}, u32[]{:S(2)}) %copy-start) | copy-done | bytes 114712
  2.2 0.0 copy-start.1
  2.2 0.8 %copy-done.1 = s32[1,128,3,32]{1,3,2,0:T(8,128)S(1)} copy-done((s32[1,128,3,32]{1,3,2,0:T(8,128)S(1)}, s32[1,128,3,32]{1,3,2,0:T(8,128)}, u32[]{:S(2)}) %copy-start.1) | copy-done | bytes 49176
  3.0 61.4 %reconstruct.1 = (f32[16,2,8,128]{3,2,1,0:T(8,128)S(1)}, f32[32,128]{1,0:T(8,128)S(1)}) custom-call(f32[7,32,128]{2,1,0:T(8,128)S(1)} %bitcast.11, s32[3,32,128]{2,1,0:T(8,128)S(1)} %bitcast.12, s32[1,128]{1,0:T(1,128)S(1)} %copy-done.2), custom_call_target="tpu_custom_call" | custom-call | tf_op jit(solution)/shard_map/reconstruct/pallas_call | solution.py:512
  64.4 0.7 %copy.7 = f32[16,16,128]{2,1,0:T(8,128)} copy(f32[16,16,128]{2,1,0:T(8,128)S(1)} %bitcast.10) | data formatting | bytes 262144
  65.0 0.6 copy.8
Async XLA Ops:
  0.6 0.7 copy-start.2
  1.3 0.9 %copy-start = (f32[1,128,7,32]{1,3,2,0:T(8,128)S(1)}, f32[1,128,7,32]{1,3,2,0:T(8,128)}, u32[]{:S(2)}) copy-start(f32[1,128,7,32]{1,3,2,0:T(8,128)} %param.3) | copy-start | bytes 344068
  2.2 0.8 %copy-start.1 = (s32[1,128,3,32]{1,3,2,0:T(8,128)S(1)}, s32[1,128,3,32]{1,3,2,0:T(8,128)}, u32[]{:S(2)}) copy-start(s32[1,128,3,32]{1,3,2,0:T(8,128)} %param.4) | copy-start | bytes 147460

commit v3 on v2

--- a/solution.py
+++ b/solution.py
@@ -38,30 +38,22 @@
     return tuple(lax.axis_index(name) for name in ("gx", "gy", "gz"))
 
 
-def coordinates(sizes, index):
-    ny, nz = sizes[1], sizes[2]
-    return (index // (ny * nz), lax.rem(index // nz, ny), lax.rem(index, nz))
-
-
 def vmem():
     return pl.BlockSpec(memory_space=pltpu.VMEM)
 
 
-def greet(sizes, here, relay_y, relay_x):
+def greet(me, meanwhile):
     barrier = pltpu.get_barrier_semaphore()
 
-    def tell(axis, semaphore):
-        for step in range(1, sizes[axis]):
-            target = tuple(lax.rem(here[a] + step, sizes[a]) if a == axis else here[a] for a in range(3))
-            pl.semaphore_signal(semaphore, inc=1, device_id=target, device_id_type=MESH)
-
-    for axis in range(3):
-        tell(axis, barrier)
-    pl.semaphore_wait(barrier, sum(sizes) - 3)
-    tell(1, relay_y)
-    pl.semaphore_wait(relay_y, sizes[1] - 1)
-    tell(0, relay_x)
-    pl.semaphore_wait(relay_x, sizes[0] - 1)
+    @pl.loop(0, DEVICES - 8, step=8)
+    def _(step):
+        for q in range(8):
+            pl.semaphore_signal(barrier, inc=1, device_id=me ^ (step + q + 1), device_id_type=pl.DeviceIdType.LOGICAL)
+
+    for q in range(DEVICES - 7, DEVICES):
+        pl.semaphore_signal(barrier, inc=1, device_id=me ^ q, device_id_type=pl.DeviceIdType.LOGICAL)
+    meanwhile()
+    pl.semaphore_wait(barrier, DEVICES - 1)
 
 
 def exchange_rows(me, send, recv, sent, send_sem, recv_sem):
@@ -244,49 +236,131 @@
             out_ref[pl.ds(group * count + q, 1), :] = value[:, q * DEVICES : (q + 1) * DEVICES]
 
 
+FACES = [(1, 0, 0), (0, 1, 0), (0, 0, 1)]
+UPPER = FACES + [(1, 1, 0), (1, 0, 1), (0, 1, 1), (1, 1, 1)]
+
+
 def roll_to(tile, source, target):
     shift = (target - source) % 128
     return pltpu.roll(tile, shift, 1) if shift else tile
 
 
+def grid_iotas():
+    lane = lax.broadcasted_iota(jnp.int32, (8, 128), 1)
+    sub = lax.broadcasted_iota(jnp.int32, (8, 128), 0)
+    return lane, sub
+
+
+def pack(read, source):
+    lane, _ = grid_iotas()
+    packed = jnp.zeros((8, 128), F32)
+    for i in range(32):
+        packed = jnp.where(lane == i, roll_to(read(i), source, i), packed)
+    return packed
+
+
+def slab_star(comb, along_x, along_y, along_z, rows, tiles):
+    n = along_y.shape[0]
+    total = comb(along_x[0:n], along_x[2 : n + 2])
+    sub3 = lax.broadcasted_iota(jnp.int32, (n, 8, 128), 1)
+    down = pltpu.roll(along_y.reshape(2 * n, 8, 128), 1, 1).reshape(n, 2, 8, 128)
+    up = pltpu.roll(along_y.reshape(2 * n, 8, 128), 7, 1).reshape(n, 2, 8, 128)
+    edge = [jnp.stack([rows(side, i) for i in range(n)]) for side in range(2)]
+    first, last = sub3 == 0, sub3 == 7
+    low = jnp.stack([jnp.where(first, edge[0], down[:, 0]), jnp.where(first, down[:, 0], down[:, 1])], axis=1)
+    high = jnp.stack([jnp.where(last, up[:, 1], up[:, 0]), jnp.where(last, edge[1], up[:, 1])], axis=1)
+    total = total + comb(low, high)
+    lanes = lax.broadcasted_iota(jnp.int32, (2 * n, 8, 128), 2)
+    flat = along_z.reshape(16 * n, 128)
+    sides = []
+    for side, shift, at in ((0, 1, 0), (1, 127, 127)):
+        edge = jnp.stack([tiles(side, i, t) for i in range(n) for t in range(2)])
+        sides.append(jnp.where(lanes == at, edge, pltpu.roll(flat, shift, 1).reshape(2 * n, 8, 128)))
+    return total + comb(*sides).reshape(n, 2, 8, 128)
+
+
+def layer_star_y(comb, side, fx, fy, fz):
+    row = lax.broadcasted_iota(jnp.int32, (16, 128), 0)
+    lane16 = lax.broadcasted_iota(jnp.int32, (16, 128), 1)
+    plane = fx["plane"][side]
+    low = jnp.where(row == 0, jnp.broadcast_to(fx["xy"][0][side], (16, 128)), pltpu.roll(plane, 1, 0))
+    high = jnp.where(row == 15, jnp.broadcast_to(fx["xy"][1][side], (16, 128)), pltpu.roll(plane, 15, 0))
+    total = comb(low, high)
+    outer, own = fy["plane2"][side], fy["own_row"][side]
+    total = total + (comb(outer, own) if side == 0 else comb(own, outer))
+    plane = fz["plane"][side]
+    parity, source = (1, 7) if side == 0 else (0, 0)
+    sides = []
+    for z_side, shift, at in ((0, 1, 0), (1, 127, 127)):
+        values = jnp.broadcast_to(fz["yz"][side][z_side][source : source + 1], (16, 128))
+        column = jnp.sum(jnp.where(lane16 == 2 * row + parity, values, 0.0), axis=1, keepdims=True)
+        sides.append(jnp.where(lane16 == at, jnp.broadcast_to(column, (16, 128)), pltpu.roll(plane, shift, 1)))
+    return total + comb(*sides)
+
+
+def layer_star_z(comb, side, fx, fy, fz):
+    lane, sub = grid_iotas()
+    layer = fx["zp"][side]
+    low = jnp.where(lane < 2, roll_to(fx["xz"][0][side], 30, 0), pltpu.roll(layer, 2, 1))
+    high = jnp.where(lane >= 30, roll_to(fx["xz"][1][side], 0, 30), pltpu.roll(layer, 126, 1))
+    total = comb(low, high)
+    layer = fy["zp"][side]
+    down, up = pltpu.roll(layer, 1, 0), pltpu.roll(layer, 7, 0)
+    odd = lax.rem(lane, 2) == 1
+    beyond = pltpu.roll(pltpu.roll(fy["yz"][0][side], 1, 0), 127, 1)
+    low = jnp.where(sub == 0, jnp.where(odd, pltpu.roll(down, 1, 1), beyond), down)
+    beyond = pltpu.roll(pltpu.roll(fy["yz"][1][side], 7, 0), 1, 1)
+    high = jnp.where(sub == 7, jnp.where(odd, beyond, pltpu.roll(up, 127, 1)), up)
+    total = total + comb(low, high)
+    outer, own = fz["zp2"][side], fz["own_z"][side]
+    total = total + (comb(outer, own) if side == 0 else comb(own, outer))
+    return jnp.where(lane < 32, total, 0.0)
+
+
 def solve(
     sizes, here, s_ref, ov_ref, u_ref, halo_ref, uz_ref,
-    m_ref, zs_ref, sx, sy, sxy, sz, p_ref, zp_ref, rx, ry, rz, r_ref, inv_ref, diag_ref,
-    fx, fy, fxy, fz, s_send, s_recv, h_send, h_recv, f_send, f_recv,
+    m_ref, zs_ref, sx, sy, sxy, sz,
+    z5, xa, xb, ya, yb, exy, za, exz, eyz,
+    pw, rw, z3, px, rx, py, py2, ry, pxy, pz, pxz, pyz, inv_ref, diag_ref, plane_ref, uzp,
+    fx, fy, fxy, fz, s_send, s_recv, g_send, g_recv, h_send, h_recv, f_send, f_recv,
 ):
     lower = [here[a] > 0 for a in range(3)]
     upper = [here[a] < sizes[a] - 1 for a in range(3)]
-    steps = [(1, 0, 0), (0, 1, 0), (0, 0, 1), (1, 1, 0), (1, 0, 1), (0, 1, 1), (1, 1, 1)]
-
-    def all_of(flags, step):
-        wanted = [flags[a] for a in range(3) if step[a]]
+
+    def present(step):
+        wanted = [(upper if step[a] > 0 else lower)[a] for a in range(3) if step[a]]
         return functools.reduce(jnp.logical_and, wanted)
 
-    def shifted(step, sign):
-        return tuple(here[a] + sign * step[a] for a in range(3))
-
-    lane = lax.broadcasted_iota(jnp.int32, (8, 128), 1)
-    sub = lax.broadcasted_iota(jnp.int32, (8, 128), 0)
+    def opposite(step):
+        return tuple(-v for v in step)
+
+    def message(step, source, target, send, recv):
+        copy = pltpu.make_async_remote_copy(
+            src_ref=source, dst_ref=target, send_sem=send, recv_sem=recv,
+            device_id=tuple(here[a] + step[a] for a in range(3)), device_id_type=MESH,
+        )
+        return step, copy
+
+    def start(messages):
+        for step, copy in messages:
+            @pl.when(present(step))
+            def _(copy=copy):
+                copy.start()
+
+    def receive(messages):
+        for step, copy in messages:
+            @pl.when(present(opposite(step)))
+            def _(copy=copy):
+                copy.wait_recv()
+
+    def drain(messages):
+        for step, copy in messages:
+            @pl.when(present(step))
+            def _(copy=copy):
+                copy.wait_send()
+
+    lane, sub = grid_iotas()
     zero = jnp.zeros((8, 128), F32)
-
-    for a, bufs in ((0, (sx, rx.at[:, 0])), (1, (sy, ry.at[:, 0])), (2, (sz.at[0], rz.at[:, 0]))):
-        @pl.when(jnp.logical_not(lower[a]))
-        def _(bufs=bufs):
-            for buf in bufs:
-                buf[...] = jnp.zeros(buf.shape, F32)
-    for a, bufs in ((0, (fx, rx.at[:, 1])), (1, (fy, ry.at[:, 1])), (2, (fz.at[0], rz.at[:, 1]))):
-        @pl.when(jnp.logical_not(upper[a]))
-        def _(bufs=bufs):
-            for buf in bufs:
-                buf[...] = jnp.zeros(buf.shape, F32)
-    for step, low_buf, high_buf in (
-        (steps[3], sxy, fxy), (steps[4], sz.at[1], fz.at[1]),
-        (steps[5], sz.at[2], fz.at[2]), (steps[6], sz.at[3], fz.at[3]),
-    ):
-        for flags, buf in ((lower, low_buf), (upper, high_buf)):
-            @pl.when(jnp.logical_not(all_of(flags, step)))
-            def _(buf=buf):
-                buf[...] = jnp.zeros(buf.shape, F32)
 
     for part, tiles in ((0, 32), (1, 5)):
         packed = zero
@@ -296,31 +370,13 @@
             here_lanes = jnp.logical_and(lane >= 4 * i, lane < 4 * i + 4)
             packed = jnp.where(here_lanes, roll_to(tile, 0, 4 * i), packed)
         zs_ref[part] = packed
+    sources = [s_ref.at[256:272], s_ref.at[272:288], zs_ref.at[0], s_ref.at[288:289]] + [zs_ref.at[1]] * 3
+    targets = [sx, sy, sz.at[0], sxy, sz.at[1], sz.at[2], sz.at[3]]
+    mass = [message(UPPER[i], sources[i], targets[i], s_send.at[i], s_recv.at[i]) for i in range(7)]
+    start(mass[::-1])
     for c in range(4):
         m_ref[c] = s_ref[0:256, 128 * c : 128 * c + 128].reshape(16, 2, 8, 128)
-
-    def corner_copies(sources, targets, send, recv, sign):
-        copies = []
-        for i, step in enumerate(steps):
-            copies.append(pltpu.make_async_remote_copy(
-                src_ref=sources[i], dst_ref=targets[i], send_sem=send.at[i], recv_sem=recv.at[i],
-                device_id=shifted(step, sign), device_id_type=MESH,
-            ))
-        return copies
-
-    def each(copies, flags, action):
-        for copy, step in zip(copies, steps):
-            @pl.when(all_of(flags, step))
-            def _(copy=copy):
-                action(copy)
-
-    mass = corner_copies(
-        [s_ref.at[256:272], s_ref.at[272:288], zs_ref.at[0], s_ref.at[288:289], zs_ref.at[1], zs_ref.at[1], zs_ref.at[1]],
-        [sx, sy, sz.at[0], sxy, sz.at[1], sz.at[2], sz.at[3]], s_send, s_recv, 1,
-    )
-    each(mass, upper, lambda copy: copy.start())
-    each(mass, lower, lambda copy: copy.wait_recv())
-
+    receive(mass)
     for c in range(4):
         columns = slice(128 * c, 128 * c + 128)
         m_ref[c, 0] += sx[:, columns].reshape(2, 8, 128)
@@ -335,116 +391,181 @@
             m_ref[c, 0, t] += jnp.where(lane == 0, roll_to(sz[1], 4 * t + c, 0), 0.0)
         corner = sxy[:, columns] + jnp.where(lane[0:1] == 0, roll_to(sz[3], 16 + c, 0)[0:1], 0.0)
         m_ref[c, 0, 0, 0:1, :] += corner
-    each(mass, upper, lambda copy: copy.wait_send())
-
-    def pack(read, source):
-        packed = zero
-        for i in range(32):
-            packed = jnp.where(lane == i, roll_to(read(i), source, i), packed)
-        return packed
-
-    def unpack(packed, target):
-        mine = lane == target
-        tiles = [jnp.where(mine, roll_to(packed, i, target), 0.0) for i in range(32)]
-        return jnp.stack(tiles).reshape(16, 2, 8, 128)
-
-    def face_copies(e, xs, ys):
-        sources = [xs.at[15], xs.at[0], ys.at[:, 1, 7, :], ys.at[:, 0, 0, :], zp_ref.at[e, 1], zp_ref.at[e, 0]]
-        targets = [rx.at[e, 0], rx.at[e, 1], ry.at[e, 0, :, 0, :], ry.at[e, 1, :, 0, :], rz.at[e, 0], rz.at[e, 1]]
-        copies = []
-        for d in range(6):
-            step = tuple(int(a == d // 2) for a in range(3))
-            copies.append(pltpu.make_async_remote_copy(
-                src_ref=sources[d], dst_ref=targets[d], send_sem=h_send.at[e, d], recv_sem=h_recv.at[e, d],
-                device_id=shifted(step, 1 - 2 * (d % 2)), device_id_type=MESH,
-            ))
-        return copies
-
-    def arriving(d):
-        return (lower, upper)[d % 2][d // 2]
-
-    def leaving(d):
-        return (upper, lower)[d % 2][d // 2]
-
-    def each_face(copies, when, action):
-        for d, copy in enumerate(copies):
-            @pl.when(when(d))
-            def _(copy=copy):
-                action(copy)
-
-    lanes4 = lax.broadcasted_iota(jnp.int32, (16, 2, 8, 128), 3)
-    subs3 = lax.broadcasted_iota(jnp.int32, (16, 8, 128), 1)
-
-    def x_sides(value, e):
-        low = jnp.concatenate([rx[e, 0][None], value[:-1]], axis=0)
-        high = jnp.concatenate([value[1:], rx[e, 1][None]], axis=0)
-        return low, high
-
-    def y_sides(value, e):
-        down = pltpu.roll(value.reshape(32, 8, 128), 1, 1).reshape(16, 2, 8, 128)
-        up = pltpu.roll(value.reshape(32, 8, 128), 7, 1).reshape(16, 2, 8, 128)
-        first = subs3 == 0
-        low = jnp.stack([jnp.where(first, ry[e, 0], down[:, 0]), jnp.where(first, down[:, 0], down[:, 1])], axis=1)
-        last = subs3 == 7
-        high = jnp.stack([jnp.where(last, up[:, 1], up[:, 0]), jnp.where(last, ry[e, 1], up[:, 1])], axis=1)
-        return low, high
-
-    def z_sides(value, e):
-        flat = value.reshape(256, 128)
-        down = pltpu.roll(flat, 1, 1).reshape(16, 2, 8, 128)
-        up = pltpu.roll(flat, 127, 1).reshape(16, 2, 8, 128)
-        low = jnp.where(lanes4 == 0, unpack(rz[e, 0], 0), down)
-        high = jnp.where(lanes4 == 127, unpack(rz[e, 1], 127), up)
-        return low, high
-
-    def pack_faces(e, read):
-        zp_ref[e, 0] = pack(read, 0)
-        zp_ref[e, 1] = pack(read, 127)
-
-    pack_faces(0, lambda i: m_ref[2, i // 2, i % 2])
-    copies = face_copies(0, m_ref.at[0], m_ref.at[1])
-    each_face(copies, leaving, lambda copy: copy.start())
-    diagonal = 6.0 + base_screen + point_screen * m_ref[3]
-    diag_ref[...] = diagonal
-    inv_ref[...] = 1.0 / diagonal
-    each_face(copies, arriving, lambda copy: copy.wait_recv())
-    low, high = x_sides(m_ref[0], 0)
-    total = high - low
-    low, high = y_sides(m_ref[1], 0)
-    total = total + (high - low)
-    low, high = z_sides(m_ref[2], 0)
-    total = -0.5 * (total + (high - low))
-    r_ref[...] = total
-    p_ref[1] = total * inv_ref[...]
-    each_face(copies, leaving, lambda copy: copy.wait_send())
-
-    for k, (keep, push) in enumerate(sweep_factors(), 1):
-        pack_faces(k, lambda i: p_ref[k, i // 2, i % 2])
-        copies = face_copies(k, p_ref.at[k], p_ref.at[k])
-        each_face(copies, leaving, lambda copy: copy.start())
-        p = p_ref[k]
-        if k == 1:
-            u_ref[...] = p
-        else:
-            u_ref[...] += p
-        each_face(copies, arriving, lambda copy: copy.wait_recv())
-        around = sum(x_sides(p, k)) + sum(y_sides(p, k)) + sum(z_sides(p, k))
-        r = r_ref[...] - (diag_ref[...] * p - around)
-        r_ref[...] = r
-        following = keep * p + push * (r * inv_ref[...])
-        if k < ITERS - 1:
-            p_ref[k + 1] = following
-        else:
-            u_ref[...] += following
-        each_face(copies, leaving, lambda copy: copy.wait_send())
-
-    zp_ref[6, 0] = pack(lambda i: u_ref[i // 2, i % 2], 0)
-    layer = corner_copies(
-        [u_ref.at[0], u_ref.at[:, 0, 0, :], zp_ref.at[6, 0], u_ref.at[0, 0, 0:1], zp_ref.at[6, 0], zp_ref.at[6, 0], zp_ref.at[6, 0]],
-        [fx, fy, fz.at[0], fxy, fz.at[1], fz.at[2], fz.at[3]], f_send, f_recv, -1,
-    )
-    each(layer, lower, lambda copy: copy.start())
-    each(layer, upper, lambda copy: copy.wait_recv())
+
+    def end(side, depth, size):
+        return size - 1 - depth if side == 0 else depth
+
+    def toward(side):
+        return 1 if side == 0 else -1
+
+    def mesh_step(**sides):
+        return tuple(toward(sides[name]) if name in sides else 0 for name in "xyz")
+
+    def numbered(entries, send, recv):
+        return [message(step, a, b, send.at[i], recv.at[i]) for i, (step, a, b) in enumerate(entries)]
+
+    for side in range(2):
+        for i, (c, depth) in enumerate(((0, 0), (2, 0), (1, 0), (3, 0), (2, 1))):
+            z5[side, i] = pack(lambda k, c=c: m_ref[c, k // 2, k % 2], end(side, depth, 128))
+    entries = []
+    for a in range(2):
+        for b in range(2):
+            entries.append((mesh_step(x=a, y=b), m_ref.at[0:2, end(a, 0, 16), 1 - b, 7 - 7 * b, :], exy.at[a, b]))
+            entries.append((mesh_step(x=a, z=b), z5.at[b, 0:2], exz.at[a, b]))
+            entries.append((mesh_step(y=a, z=b), z5.at[b, 1:3], eyz.at[a, b]))
+    for a in range(2):
+        first = 14 if a == 0 else 0
+        entries.append((mesh_step(x=a), m_ref.at[0, first : first + 2], xa.at[a]))
+        entries.append((mesh_step(x=a), m_ref.at[1:4, end(a, 0, 16)], xb.at[a]))
+        entries.append((mesh_step(y=a), m_ref.at[:, :, 1 - a, 7 - 7 * a, :], ya.at[a]))
+        entries.append((mesh_step(y=a), m_ref.at[1, :, 1 - a, 6 - 5 * a, :], yb.at[a]))
+        entries.append((mesh_step(z=a), z5.at[a], za.at[a]))
+    ghost = numbered(entries, g_send, g_recv)
+    start(ghost)
+    receive(ghost)
+
+    def tiles_of(zp, xz):
+        def tiles(side, i, t):
+            at = 0 if side == 0 else 127
+            if i == 0:
+                return roll_to(xz[0][side], 30 + t, at)
+            if i == 17:
+                return roll_to(xz[1][side], t, at)
+            return roll_to(zp[side], 2 * (i - 1) + t, at)
+        return tiles
+
+    def rows_of(row, xy):
+        def rows(side, i):
+            value = xy[0][side] if i == 0 else xy[1][side] if i == 17 else row(side, i - 1)
+            return jnp.broadcast_to(value, (8, 128))
+        return rows
+
+    def both(get):
+        return [get(0), get(1)]
+
+    def grid2(get):
+        return [[get(a, b) for b in range(2)] for a in range(2)]
+
+    def difference(low, high):
+        return high - low
+
+    def plus(low, high):
+        return low + high
+
+    nx = {
+        "plane": both(lambda a: ya[a, 0]), "xy": grid2(lambda a, b: exy[a, b, 0:1]),
+        "zp": both(lambda a: za[a, 0]), "xz": grid2(lambda a, b: exz[a, b, 0]),
+    }
+    ny = {
+        "plane2": both(lambda a: yb[a]), "own_row": both(lambda a: m_ref[1, :, a, 7 * a, :]),
+        "zp": both(lambda a: za[a, 2]), "yz": grid2(lambda a, b: eyz[a, b, 1]),
+    }
+    nz = {
+        "plane": both(lambda a: ya[a, 2]), "yz": grid2(lambda a, b: eyz[a, b, 0]),
+        "zp2": both(lambda a: za[a, 4]), "own_z": both(lambda a: z5[1 - a, 1]),
+    }
+    along_x = jnp.concatenate([xa[0], m_ref[0], xa[1]], axis=0)
+    along_y = jnp.concatenate([xb[0, 0:1], m_ref[1], xb[1, 0:1]], axis=0)
+    along_z = jnp.concatenate([xb[0, 1:2], m_ref[2], xb[1, 1:2]], axis=0)
+    rows = rows_of(lambda side, x: ya[side, 1, x : x + 1, :], grid2(lambda a, b: exy[a, b, 1:2]))
+    tiles = tiles_of(both(lambda a: za[a, 1]), grid2(lambda a, b: exz[a, b, 1]))
+    source = -0.5 * slab_star(difference, along_x, along_y, along_z, rows, tiles)
+
+    def shift_diagonal(mass_part):
+        return 6.0 + base_screen + point_screen * mass_part
+
+    def inverse(diagonal, exists):
+        return jnp.where(exists, 1.0 / diagonal, 0.0)
+
+    slabs = shift_diagonal(jnp.concatenate([xb[0, 2:3], m_ref[3], xb[1, 2:3]], axis=0))
+    diag_ref[...] = slabs
+    inv_ref[0] = inverse(slabs[0], lower[0])
+    inv_ref[1:17] = 1.0 / slabs[1:17]
+    inv_ref[17] = inverse(slabs[17], upper[0])
+    exists = lambda axis, side: (lower, upper)[side][axis]
+    diag_y = both(lambda a: shift_diagonal(ya[a, 3]))
+    inv_y = both(lambda a: inverse(diag_y[a], exists(1, a)))
+    diag_z = both(lambda a: shift_diagonal(za[a, 3]))
+    inv_z = both(lambda a: inverse(diag_z[a], exists(2, a)))
+
+    def second_sweep(round_index, slabs, planes, layers, residual, keep, push):
+        for side in range(2):
+            plane_ref[round_index, side] = planes[side]
+        own = slabs[1:17]
+        around = slab_star(
+            plus, slabs, own, own,
+            lambda side, i: jnp.broadcast_to(plane_ref[round_index, side, i : i + 1, :], (8, 128)),
+            lambda side, i, t: roll_to(layers[side], 2 * i + t, 0 if side == 0 else 127),
+        )
+        residual = residual - (diag_ref[1:17] * own - around)
+        return residual, keep * own + push * (residual * inv_ref[1:17])
+
+    factors = sweep_factors()
+    slabs = source * inv_ref[...]
+    planes = both(lambda a: -0.5 * layer_star_y(difference, a, nx, ny, nz) * inv_y[a])
+    layers = both(lambda a: -0.5 * layer_star_z(difference, a, nx, ny, nz) * inv_z[a])
+    u_ref[...] = slabs[1:17]
+    residual, following = second_sweep(0, slabs, planes, layers, source[1:17], *factors[0])
+
+    rounds = []
+    for e in range(2):
+        pw[e] = following
+        rw[e] = residual
+        for side in range(2):
+            for i, (ref, depth) in enumerate(((pw, 0), (pw, 1), (rw, 0))):
+                z3[e, side, i] = pack(lambda k, ref=ref: ref[e, k // 2, k % 2], end(side, depth, 128))
+        entries = []
+        for a in range(2):
+            for b in range(2):
+                row = pw.at[e, end(a, 0, 16), 1 - b, 7 - 7 * b : 8 - 7 * b, :]
+                entries.append((mesh_step(x=a, y=b), row, pxy.at[e, a, b]))
+                entries.append((mesh_step(x=a, z=b), z3.at[e, b, 0], pxz.at[e, a, b]))
+                entries.append((mesh_step(y=a, z=b), z3.at[e, b, 0], pyz.at[e, a, b]))
+        for a in range(2):
+            first = 14 if a == 0 else 0
+            entries.append((mesh_step(x=a), pw.at[e, first : first + 2], px.at[e, a]))
+            entries.append((mesh_step(x=a), rw.at[e, end(a, 0, 16)], rx.at[e, a]))
+            entries.append((mesh_step(y=a), pw.at[e, :, 1 - a, 7 - 7 * a, :], py.at[e, a]))
+            entries.append((mesh_step(y=a), pw.at[e, :, 1 - a, 6 - 5 * a, :], py2.at[e, a]))
+            entries.append((mesh_step(y=a), rw.at[e, :, 1 - a, 7 - 7 * a, :], ry.at[e, a]))
+            entries.append((mesh_step(z=a), z3.at[e, a], pz.at[e, a]))
+        ghosts = numbered(entries, h_send.at[e], h_recv.at[e])
+        rounds.append(ghosts)
+        start(ghosts)
+        u_ref[...] += following
+        receive(ghosts)
+        p = {
+            "plane": both(lambda a: py[e, a]), "plane2": both(lambda a: py2[e, a]),
+            "own_row": both(lambda a: pw[e, :, a, 7 * a, :]), "xy": grid2(lambda a, b: pxy[e, a, b]),
+            "zp": both(lambda a: pz[e, a, 0]), "zp2": both(lambda a: pz[e, a, 1]),
+            "own_z": both(lambda a: z3[e, 1 - a, 0]),
+            "xz": grid2(lambda a, b: pxz[e, a, b]), "yz": grid2(lambda a, b: pyz[e, a, b]),
+        }
+        wide = jnp.concatenate([px[e, 0], pw[e], px[e, 1]], axis=0)
+        middle = wide[1:19]
+        rows = rows_of(lambda side, x: py[e, side, x : x + 1, :], p["xy"])
+        around = slab_star(plus, wide, middle, middle, rows, tiles_of(p["zp"], p["xz"]))
+        residual = jnp.concatenate([rx[e, 0][None], rw[e], rx[e, 1][None]], axis=0)
+        residual = residual - (diag_ref[...] * middle - around)
+        keep, push = factors[2 * e + 1]
+        slabs = keep * middle + push * (residual * inv_ref[...])
+
+        def outside(own, rest, diagonal, inverse_diagonal, star):
+            rest = rest - (diagonal * own - star)
+            return keep * own + push * (rest * inverse_diagonal)
+
+        planes = both(lambda a: outside(p["plane"][a], ry[e, a], diag_y[a], inv_y[a], layer_star_y(plus, a, p, p, p)))
+        layers = both(lambda a: outside(p["zp"][a], pz[e, a, 2], diag_z[a], inv_z[a], layer_star_z(plus, a, p, p, p)))
+        u_ref[...] += slabs[1:17]
+        residual, following = second_sweep(e + 1, slabs, planes, layers, residual[1:17], *factors[2 * e + 2])
+    u_ref[...] += following
+
+    uzp[...] = pack(lambda i: u_ref[i // 2, i % 2], 0)
+    sources = [u_ref.at[0], u_ref.at[:, 0, 0, :], uzp, u_ref.at[0, 0, 0:1]] + [uzp] * 3
+    targets = [fx, fy, fz.at[0], fxy, fz.at[1], fz.at[2], fz.at[3]]
+    layer = [message(opposite(UPPER[i]), sources[i], targets[i], f_send.at[i], f_recv.at[i]) for i in range(7)]
+    start(layer[::-1])
+    receive(layer)
     halo_ref[0:16] = fx[...].reshape(16, 128)
     halo_ref[16:32] = fy[...]
     halo_ref[32:40] = jnp.where(sub == 0, jnp.broadcast_to(fxy[...], (8, 128)), 0.0)
@@ -458,25 +579,44 @@
         uz_ref[272 + 8 * t : 280 + 8 * t] = jnp.broadcast_to(column, (8, 128))
     uz_ref[288:296] = jnp.where(sub == 0, fz[3], 0.0)
     uz_ref[296:304] = zero
-    each(layer, lower, lambda copy: copy.wait_send())
+    for messages in (mass, ghost, *rounds, layer):
+        drain(messages)
+
+
+FIELD = (16, 2, 8, 128)
+SOLVE_SHAPES = [
+    (4, *FIELD), (2, 8, 128), (16, 512), (16, 512), (1, 512), (4, 8, 128),
+    (2, 5, 8, 128), (2, 2, 2, 8, 128), (2, 3, 2, 8, 128), (2, 4, 16, 128), (2, 16, 128), (2, 2, 2, 128),
+    (2, 5, 8, 128), (2, 2, 2, 8, 128), (2, 2, 2, 8, 128),
+    (2, *FIELD), (2, *FIELD), (2, 2, 3, 8, 128), (2, 2, 2, 2, 8, 128), (2, 2, 2, 8, 128),
+    (2, 2, 16, 128), (2, 2, 16, 128), (2, 2, 16, 128), (2, 2, 2, 1, 128), (2, 2, 3, 8, 128),
+    (2, 2, 2, 8, 128), (2, 2, 2, 8, 128), (18, 2, 8, 128), (18, 2, 8, 128), (3, 2, 16, 128), (8, 128),
+    (2, 8, 128), (16, 128), (1, 128), (4, 8, 128),
+]
+LANDING = [2, 3, 4, 5, 7, 8, 9, 10, 11, 12, 13, 14, 18, 19, 20, 21, 22, 23, 24, 25, 26, 31, 32, 33, 34]
 
 
 def kernel(sizes, data_hbm, cells_hbm, counts_hbm, u_ref, out_ref, *scratch):
     (data_ref, cells_ref, counts_ref, send, recv, sent, d_ref, a0, b0, a1, b1, acc_ref, ov_ref,
      l_ref, r_ref, halo_ref, uz_ref, val_ref, back_send, back_recv, back_sent,
-     in_sem, send_sem, recv_sem, relay_y, relay_x, *rest) = scratch
+     in_sem, send_sem, recv_sem, *rest) = scratch
     here = position(sizes)
     me = (here[0] * sizes[1] + here[1]) * sizes[2] + here[2]
+    for at in LANDING:
+        rest[at][...] = jnp.zeros(rest[at].shape, F32)
     loads = [
         pltpu.make_async_copy(source, target, in_sem.at[i])
         for i, (source, target) in enumerate(((data_hbm, data_ref), (cells_hbm, cells_ref), (counts_hbm, counts_ref)))
     ]
     for load in loads:
         load.start()
-    for load in loads:
-        load.wait()
-    prepare_rows(data_ref, cells_ref, counts_ref, send)
-    greet(sizes, here, relay_y, relay_x)
+
+    def meanwhile():
+        for load in loads:
+            load.wait()
+        prepare_rows(data_ref, cells_ref, counts_ref, send)
+
+    greet(me, meanwhile)
     exchange_rows(me, send, recv, sent, send_sem.at[0], recv_sem.at[0])
     d_ref[...] = recv[...].T[: CAP * CHANNELS].reshape(CHANNELS, CAP, DEVICES)
     splat_points(d_ref, acc_ref, ov_ref, a0, b0, a1, b1)
@@ -494,8 +634,7 @@
 def on_device(sizes, point_data, point_cells, send_counts):
     data = jnp.transpose(point_data[0], (1, 2, 0))
     cells = jnp.transpose(point_cells[0], (1, 2, 0))
-    dma, regular = pltpu.SemaphoreType.DMA, pltpu.SemaphoreType.REGULAR
-    field = (16, 2, 8, 128)
+    dma = pltpu.SemaphoreType.DMA
     shapes = [
         ((7, CAP, DEVICES), F32), ((3, CAP, DEVICES), jnp.int32), ((1, DEVICES), jnp.int32),
         ((DEVICES, WIDTH), F32), ((DEVICES, WIDTH), F32), ((1, WIDTH), F32), ((CHANNELS, CAP, DEVICES), F32),
@@ -504,25 +643,20 @@
         ((48, 128), F32), ((ROWS, 128), F32), ((CAP, DEVICES), F32),
         ((DEVICES, DEVICES), F32), ((DEVICES, DEVICES), F32), ((1, DEVICES), F32),
     ]
-    halo_shapes = [
-        (4, *field), (2, 8, 128), (16, 512), (16, 512), (1, 512), (4, 8, 128),
-        (6, *field), (7, 2, 8, 128), (6, 2, 2, 8, 128), (6, 2, 16, 1, 128), (6, 2, 8, 128), field, field, field,
-        (2, 8, 128), (16, 128), (1, 128), (4, 8, 128),
-    ]
     u, returned = pl.pallas_call(
         functools.partial(kernel, sizes),
-        out_shape=[jax.ShapeDtypeStruct(s, F32) for s in (field, (CAP, DEVICES))],
-        in_specs=[pl.BlockSpec(memory_space=pl.ANY)] * 3,
+        out_shape=[jax.ShapeDtypeStruct(s, F32) for s in (FIELD, (CAP, DEVICES))],
+        in_specs=[pl.BlockSpec(memory_space=pltpu.HBM)] * 3,
         out_specs=[vmem()] * 2,
         scratch_shapes=[pltpu.VMEM(*s) for s in shapes]
-        + [dma((3,)), dma((2,)), dma((2,)), regular, regular]
-        + [pltpu.VMEM(s, F32) for s in halo_shapes]
-        + [dma((7,)), dma((7,)), dma((6, 6)), dma((6, 6)), dma((7,)), dma((7,))],
+        + [dma((3,)), dma((2,)), dma((2,))]
+        + [pltpu.VMEM(s, F32) for s in SOLVE_SHAPES]
+        + [dma((7,)), dma((7,)), dma((22,)), dma((22,)), dma((2, 24)), dma((2, 24)), dma((7,)), dma((7,))],
         compiler_params=pltpu.CompilerParams(
             vmem_limit_bytes=24 * 1024 * 1024, collective_id=0, has_side_effects=True
         ),
         name="reconstruct",
-    )(data, cells, send_counts)
+    )(*[pltpu.with_memory_space_constraint(v, pltpu.HBM) for v in (data, cells, send_counts)])
     return u.reshape(16, 16, 128), returned.T[None]
 
 

time: 65.8 us -> 56.4 us (0.86)
  Pallas kernels: 61.4 us -> 54.4 us
  local copies, waits for them, and re-layouts: 3.61 us -> 1.26 us
    pallas_call x1, Pallas kernels: 61.4 us -> 54.4 us  [on_device(): pl.pallas_call(functools.partial(kernel, sizes), out_shape=[jax.ShapeDtyp...]
    unnamed x8 -> x2, local copies, waits for them, and re-layouts: 3.61 us -> 1.26 us
where the time goes in v3:
time: 56.4 us; the launch traced here: 56.3 us
  Pallas kernels  54.4 us (96%)
  local copies, waits for them, and re-layouts  1.26 us (2%)
  between operations  0.64 us (1%)
    pallas_call x1, Pallas kernels, on_device(): pl.pallas_call(functools.partial(kernel, sizes), out_shape=[jax.ShapeDtyp...  54.4 us
    unnamed x2, local copies, waits for them, and re-layouts  1.26 us

profile of v3, /device:TPU:1, one launch (start us, length us, event | category | flops | bytes accessed | tf_op | source)
XLA Modules:
  0.0 56.3 jit_solution(13669344147468678913)
XLA Ops:
  0.6 54.4 %reconstruct.1 = (f32[16,2,8,128]{3,2,1,0:T(8,128)S(1)}, f32[32,128]{1,0:T(8,128)S(1)}) custom-call(f32[7,32,128]{2,1,0:T(8,128)} %bitcast.12, s32[3,32,128]{2,1,0:T(8,128)} %bitcast.13, s32[1,128]{1,0:T(1,128)} %counts_hbm.1), custom_call_target="tpu_custom_call" | custom-call | tf_op jit(solution)/shard_map/reconstruct/pallas_call | solution.py:646
  55.1 0.7 %copy.7 = f32[16,16,128]{2,1,0:T(8,128)} copy(f32[16,16,128]{2,1,0:T(8,128)S(1)} %bitcast.10) | data formatting | bytes 262144
  55.7 0.6 %copy.8 = f32[1,128,32]{1,2,0:T(8,128)} copy(f32[1,128,32]{1,2,0:T(8,128)S(1)} %bitcast.11) | data formatting | bytes 32768

commit v4 on v3

--- a/solution.py
+++ b/solution.py
@@ -18,6 +18,7 @@
 POINTS = 512
 ROWS = 304
 ITERS = 6
+GROUPS = CAP * DEVICES // POINTS
 
 base_screen = 0.25
 point_screen = 4.0
@@ -94,146 +95,185 @@
     return high, (value - high.astype(F32)).astype(BF16)
 
 
-def point_rows(d_ref, group, channel):
-    count = POINTS // DEVICES
-    rows = [d_ref[channel, pl.ds(group * count + q, 1), :] for q in range(count)]
-    return jnp.concatenate(rows, axis=1)
-
-
-def spread(row):
-    return jnp.broadcast_to(row, (16, POINTS)).astype(BF16)
-
-
-def spread_split(row):
-    wide = jnp.broadcast_to(row, (16, POINTS))
-    return split(wide)
-
-
-def build_tiles(d_ref, group, a_ref, b_ref):
-    iota = lax.broadcasted_iota(jnp.int32, (16, POINTS), 0).astype(F32).astype(BF16)
-    zero = jnp.zeros((16, POINTS), BF16)
-
-    def store_a(first, high, low):
-        rows = pl.ds(first, 16)
-        a_ref[rows, 0:POINTS] = high
-        a_ref[rows, POINTS : 2 * POINTS] = low
-        a_ref[rows, 2 * POINTS : 3 * POINTS] = high
-
-    def store_b(first, high, low):
-        rows = pl.ds(first, 16)
-        b_ref[rows, 0:POINTS] = high
-        b_ref[rows, POINTS : 2 * POINTS] = high
-        b_ref[rows, 2 * POINTS : 3 * POINTS] = low
-
-    v = [point_rows(d_ref, group, c) for c in range(4)]
-    fx, fy, fz, cx, cy, cz = [point_rows(d_ref, group, 4 + c) for c in range(6)]
-    bx, by, bz = spread(cx), spread(cy), spread(cz)
-    y0, y1 = by == iota, (by + 1.0).astype(BF16) == iota
-    near = [], []
-    for along, out in ((1.0 - fx, 0), (fx, 1)):
-        w0 = spread_split(along * (1.0 - fy))
-        w1 = spread_split(along * fy)
+WIDE = 256
+
+
+def lane_rows(d_ref, group, block, channels):
+    first = (group * POINTS + block * WIDE) // DEVICES
+    wide = lambda c, q: jnp.broadcast_to(d_ref[c, pl.ds(first + q, 1), :], (16, DEVICES))
+    return [jnp.concatenate([wide(c, q) for q in range(WIDE // DEVICES)], axis=1) for c in channels]
+
+
+def tile_iota():
+    return lax.broadcasted_iota(jnp.int32, (16, WIDE), 0).astype(F32).astype(BF16)
+
+
+def build_block(d_ref, group, block, a_ref, b_ref):
+    iota = tile_iota()
+    zero = jnp.zeros((16, WIDE), BF16)
+    lanes = slice(block * WIDE, (block + 1) * WIDE)
+    v = lane_rows(d_ref, group, block, range(4))
+    fx, fy, fz, cx, cy, cz = lane_rows(d_ref, group, block, range(4, 10))
+    bz = cz.astype(BF16)
+    bz1 = (cz + 1.0).astype(BF16)
+    g0 = [split(v[c] * (1.0 - fz)) for c in range(4)]
+    g1 = [split(v[c] * fz) for c in range(4)]
+    for t in range(8):
+        at = iota + jnp.asarray(16 * t, BF16)
+        z0, z1 = bz == at, bz1 == at
+        for c in range(4):
+            for part in range(2):
+                value = jnp.where(z0, g0[c][part], jnp.where(z1, g1[c][part], zero))
+                b_ref[512 * part + 128 * c + 16 * t : 512 * part + 128 * c + 16 * t + 16, lanes] = value
+    top = bz == 127
+    both = zero
+    for c in range(4):
         for part in range(2):
-            near[out].append(jnp.where(y0, w0[part], jnp.where(y1, w1[part], zero)))
+            both = jnp.where(iota == c + 4 * part, g1[c][part], both)
+    b_ref[1024:1040, lanes] = jnp.where(top, both, zero)
+    by, by1 = cy.astype(BF16), (cy + 1.0).astype(BF16)
+    y0, y1 = by == iota, by1 == iota
+    near, far = [], []
+    for along, out in ((1.0 - fx, near), (fx, far)):
+        w0, w1 = split(along * (1.0 - fy)), split(along * fy)
+        for part in range(2):
+            out.append(jnp.where(y0, w0[part], jnp.where(y1, w1[part], zero)))
+    bx = cx.astype(BF16)
+    below = None
     for x in range(17):
-        x0, x1 = bx == x, bx == x - 1
-        high, low = [jnp.where(x0, near[0][part], jnp.where(x1, near[1][part], zero)) for part in range(2)]
-        store_a(16 * x, high, low)
+        here = bx == x
+        for part in range(2):
+            value = near[part] if below is None else jnp.where(below, far[part], zero)
+            value = jnp.where(here, near[part], zero if below is None else value)
+            first = (256 * part + 16 * x) if x < 16 else 512 + 48 * part
+            a_ref[first : first + 16, lanes] = value
+        below = here
+    bx1 = (cx + 1.0).astype(BF16)
     edge = jnp.where(cy == 15.0, fy, 0.0)
-    e0, e1 = spread_split((1.0 - fx) * edge), spread_split(fx * edge)
+    e0, e1 = split((1.0 - fx) * edge), split(fx * edge)
     for t in range(2):
         at = iota + jnp.asarray(16 * t, BF16)
-        x0, x1 = bx == at, (bx + 1.0).astype(BF16) == at
-        high, low = [jnp.where(x0, e0[part], jnp.where(x1, e1[part], zero)) for part in range(2)]
-        store_a(272 + 16 * t, high, low)
-    g0 = [spread_split(v[c] * (1.0 - fz)) for c in range(4)]
-    g1 = [spread_split(v[c] * fz) for c in range(4)]
-    for t in range(8):
-        at = iota + jnp.asarray(16 * t, BF16)
-        z0, z1 = bz == at, (bz + 1.0).astype(BF16) == at
-        for c in range(4):
-            high, low = [jnp.where(z0, g0[c][part], jnp.where(z1, g1[c][part], zero)) for part in range(2)]
-            store_b(128 * c + 16 * t, high, low)
-    top = bz == 127
-    high, both = zero, zero
-    for c in range(4):
-        here = jnp.logical_and(top, iota == c)
-        high = jnp.where(here, g1[c][0], high)
-        both = jnp.where(jnp.logical_and(top, iota == c + 4), g1[c][1], both)
-    b_ref[512:528, 0:POINTS] = jnp.where(iota < 4, high, both)
-    b_ref[512:528, POINTS : 2 * POINTS] = high
-
-
-def multiply_tiles(a_ref, b_ref, acc_ref, ov_ref):
-    dims = (((1,), (1,)), ((), ()))
-    acc_ref[...] += lax.dot_general(a_ref[...], b_ref[0:512, :], dims, preferred_element_type=F32)
-    ov_ref[:, 0:16] += lax.dot_general(
-        a_ref[:, 0 : 2 * POINTS], b_ref[512:528, 0 : 2 * POINTS], dims, preferred_element_type=F32
-    )
-
-
-def splat_points(d_ref, acc_ref, ov_ref, a0, b0, a1, b1):
+        x0, x1 = bx == at, bx1 == at
+        for part in range(2):
+            first = 528 + 48 * part + 16 * t
+            a_ref[first : first + 16, lanes] = jnp.where(x0, e0[part], jnp.where(x1, e1[part], zero))
+
+
+ROW_DIMS = (((1,), (1,)), ((), ()))
+
+
+def rows_by_rows(left, right):
+    return lax.dot_general(left, right, ROW_DIMS, preferred_element_type=F32)
+
+
+def multiply_outside(piece, a_ref, b_ref, acc_ref, ov_ref):
+    if piece == 0:
+        acc_ref[512:608, 0:256] += rows_by_rows(a_ref[512:608, :], b_ref[0:256, :])
+    elif piece == 1:
+        acc_ref[512:608, 256:512] += rows_by_rows(a_ref[512:608, :], b_ref[256:512, :])
+    elif piece == 2:
+        acc_ref[512:560, :] += rows_by_rows(a_ref[512:560, :], b_ref[512:1024, :])
+    else:
+        ov_ref[:, 0:16] += rows_by_rows(a_ref[...], b_ref[1024:1040, :])
+
+
+def splat_outside(d_ref, acc_ref, ov_ref, a_refs, b_refs):
     acc_ref[...] = jnp.zeros_like(acc_ref)
     ov_ref[...] = jnp.zeros_like(ov_ref)
-    groups = CAP * DEVICES // POINTS
-    build_tiles(d_ref, 0, a0, b0)
-
-    @pl.loop(0, groups // 2)
-    def _(pair):
-        build_tiles(d_ref, 2 * pair + 1, a1, b1)
-        multiply_tiles(a0, b0, acc_ref, ov_ref)
-        build_tiles(d_ref, jnp.minimum(2 * pair + 2, groups - 1), a0, b0)
-        multiply_tiles(a1, b1, acc_ref, ov_ref)
-
-
-def interpolate(d_ref, u_ref, halo_ref, uz_ref, out_ref, l_ref, r_ref):
-    for first, value in ((0, u_ref[...].reshape(256, 128)), (256, halo_ref[...])):
-        rows = pl.ds(first, value.shape[0])
-        high, low = split(value)
-        l_ref[rows, 0:128] = high
-        l_ref[rows, 128:256] = low
-        l_ref[rows, 256:384] = high
+    for block in range(POINTS // WIDE):
+        build_block(d_ref, 0, block, a_refs[0], b_refs[0])
+    for group in range(GROUPS):
+        for block in range(4):
+            if group + 1 < GROUPS and block < POINTS // WIDE:
+                build_block(d_ref, group + 1, block, a_refs[group + 1], b_refs[group + 1])
+            multiply_outside(block, a_refs[group], b_refs[group], acc_ref, ov_ref)
+
+
+def splat_inside(acc_ref, a_refs, b_refs):
+    for a_ref, b_ref in zip(a_refs, b_refs):
+        acc_ref[0:512, :] += rows_by_rows(a_ref[0:512, :], b_ref[0:512, :])
+        acc_ref[0:256, :] += rows_by_rows(a_ref[0:256, :], b_ref[512:1024, :])
+
+
+def interpolation_tables(d_ref, r_ref, w_ref):
+    iota = tile_iota()
+    iota_f = iota.astype(F32)
+    zero = jnp.zeros((16, WIDE), BF16)
+
+    @pl.loop(0, GROUPS)
+    def _(group):
+        r_ref[group, 400:512, :] = jnp.zeros((112, POINTS), BF16)
+        for block in range(POINTS // WIDE):
+            lanes = slice(block * WIDE, (block + 1) * WIDE)
+            fx, fy, fz, cx, cy, cz = lane_rows(d_ref, group, block, range(4, 10))
+            bz, bz1 = cz.astype(BF16), (cz + 1.0).astype(BF16)
+            g0, g1 = split(1.0 - fz), split(fz)
+            for t in range(8):
+                at = iota + jnp.asarray(16 * t, BF16)
+                z0, z1 = bz == at, bz1 == at
+                high, low = [jnp.where(z0, g0[part], jnp.where(z1, g1[part], zero)) for part in range(2)]
+                r_ref[group, 16 * t : 16 * t + 16, lanes] = high
+                r_ref[group, 128 + 16 * t : 144 + 16 * t, lanes] = high
+                r_ref[group, 256 + 16 * t : 272 + 16 * t, lanes] = low
+            picked = jnp.where(iota <= 1, g1[0], jnp.where(iota == 2, g1[1], zero))
+            r_ref[group, 384:400, lanes] = jnp.where(bz == 127, picked, zero)
+            hat_y = jnp.where(cy == iota_f, 1.0 - fy, jnp.where(cy + 1.0 == iota_f, fy, 0.0))
+            near, far = (1.0 - fx) * hat_y, fx * hat_y
+            for x in range(17):
+                w_ref[group, 16 * x : 16 * x + 16, lanes] = jnp.where(cx == x, near, jnp.where(cx == x - 1, far, 0.0))
+            edge = jnp.where(cy == 15.0, fy, 0.0)
+            for t in range(2):
+                at = iota_f + 16.0 * t
+                hat = jnp.where(cx == at, 1.0 - fx, jnp.where(cx + 1.0 == at, fx, 0.0))
+                w_ref[group, 272 + 16 * t : 288 + 16 * t, lanes] = hat * edge
+
+
+def weighted(g, w_ref, group, first):
+    rows = g.shape[0]
+    total = g[0:8] * w_ref[group, first : first + 8]
+    for i in range(1, rows // 8):
+        total = total + g[8 * i : 8 * i + 8] * w_ref[group, first + 8 * i : first + 8 * i + 8]
+    return total
+
+
+def high_and_low(l_ref, first, value):
+    rows = pl.ds(first, value.shape[0])
+    high, low = split(value)
+    l_ref[rows, 0:128] = high
+    l_ref[rows, 128:256] = low
+    l_ref[rows, 256:384] = high
+
+
+def interpolate_inside(u_ref, part_ref, l_ref, r_ref, w_ref):
+    high_and_low(l_ref, 0, u_ref[...].reshape(256, 128))
+
+    @pl.loop(0, GROUPS, step=4)
+    def _(first):
+        for step in range(4):
+            group = first + step
+            g = jnp.dot(l_ref[0:256, 0:384], r_ref[group, 0:384], preferred_element_type=F32)
+            part_ref[group] = weighted(g, w_ref, group, 0)
+
+
+def interpolate(halo_ref, uz_ref, part_ref, out_ref, l_ref, r_ref, w_ref):
+    high_and_low(l_ref, 256, halo_ref[...])
     top = jnp.broadcast_to(uz_ref[:, 0:1], (ROWS, 128))
     high = top.astype(BF16).astype(F32)
     lane = lax.broadcasted_iota(jnp.int32, (ROWS, 128), 1)
     low = jnp.where(lane == 1, top - high, 0.0)
     l_ref[:, 384:512] = jnp.where(jnp.logical_or(lane == 0, lane == 2), high, low).astype(BF16)
-    r_ref[400:512, :] = jnp.zeros((112, POINTS), BF16)
-    iota_f = lax.broadcasted_iota(jnp.int32, (16, POINTS), 0).astype(F32)
-    iota = iota_f.astype(BF16)
-    zero = jnp.zeros((16, POINTS), BF16)
-
-    @pl.loop(0, CAP * DEVICES // POINTS)
-    def _(group):
-        fx, fy, fz, cx, cy, cz = [point_rows(d_ref, group, 4 + c) for c in range(6)]
-        bz = spread(cz)
-        g0, g1 = spread_split(1.0 - fz), spread_split(fz)
-        for t in range(8):
-            at = iota + jnp.asarray(16 * t, BF16)
-            z0, z1 = bz == at, (bz + 1.0).astype(BF16) == at
-            high, low = [jnp.where(z0, g0[part], jnp.where(z1, g1[part], zero)) for part in range(2)]
-            r_ref[pl.ds(16 * t, 16), :] = high
-            r_ref[pl.ds(128 + 16 * t, 16), :] = high
-            r_ref[pl.ds(256 + 16 * t, 16), :] = low
-        top = bz == 127
-        high = jnp.where(jnp.logical_and(top, iota <= 1), g1[0], zero)
-        r_ref[384:400, :] = jnp.where(jnp.logical_and(top, iota == 2), g1[1], high)
-        g = jnp.dot(l_ref[...], r_ref[...], preferred_element_type=F32)
-        total = jnp.zeros((16, POINTS), F32)
-        for x in range(17):
-            hat = jnp.where(cx == x, 1.0 - fx, jnp.where(cx == x - 1, fx, 0.0))
-            total = total + hat * g[16 * x : 16 * x + 16]
-        hat = jnp.where(cy == iota_f, 1.0 - fy, jnp.where(cy + 1.0 == iota_f, fy, 0.0))
-        total = total * hat
-        edge = jnp.where(cy == 15.0, fy, 0.0)
-        for t in range(2):
-            at = iota_f + 16.0 * t
-            hat = jnp.where(cx == at, 1.0 - fx, jnp.where(cx + 1.0 == at, fx, 0.0))
-            total = total + hat * edge * g[272 + 16 * t : 288 + 16 * t]
-        value = jnp.sum(total, axis=0, keepdims=True)
-        count = POINTS // DEVICES
-        for q in range(count):
-            out_ref[pl.ds(group * count + q, 1), :] = value[:, q * DEVICES : (q + 1) * DEVICES]
+
+    @pl.loop(0, GROUPS, step=4)
+    def _(first):
+        for step in range(4):
+            group = first + step
+            g = jnp.dot(l_ref[256:ROWS, :], r_ref[group], preferred_element_type=F32)
+            total = part_ref[group] + weighted(g, w_ref, group, 256)
+            g = jnp.dot(l_ref[0:256, 384:512], r_ref[group, 384:512], preferred_element_type=F32)
+            value = jnp.sum(total + weighted(g, w_ref, group, 0), axis=0, keepdims=True)
+            count = POINTS // DEVICES
+            for q in range(count):
+                out_ref[pl.ds(group * count + q, 1), :] = value[:, q * DEVICES : (q + 1) * DEVICES]
 
 
 FACES = [(1, 0, 0), (0, 1, 0), (0, 0, 1)]
@@ -318,7 +358,7 @@
 
 
 def solve(
-    sizes, here, s_ref, ov_ref, u_ref, halo_ref, uz_ref,
+    sizes, here, own_rows, tables, own_values, s_ref, ov_ref, out_ref, u_ref, halo_ref, uz_ref,
     m_ref, zs_ref, sx, sy, sxy, sz,
     z5, xa, xb, ya, yb, exy, za, exz, eyz,
     pw, rw, z3, px, rx, py, py2, ry, pxy, pz, pxz, pyz, inv_ref, diag_ref, plane_ref, uzp,
@@ -365,17 +405,21 @@
     for part, tiles in ((0, 32), (1, 5)):
         packed = zero
         for i in range(tiles):
-            tile = ov_ref[pl.ds(256 * part + 8 * i, 8), :]
+            first = 512 * part + 8 * i
+            tile = ov_ref[pl.ds(first, 8), :] + ov_ref[pl.ds(first + (48 if part else 256), 8), :]
             tile = tile + pltpu.roll(tile, 124, 1)
             here_lanes = jnp.logical_and(lane >= 4 * i, lane < 4 * i + 4)
             packed = jnp.where(here_lanes, roll_to(tile, 0, 4 * i), packed)
         zs_ref[part] = packed
-    sources = [s_ref.at[256:272], s_ref.at[272:288], zs_ref.at[0], s_ref.at[288:289]] + [zs_ref.at[1]] * 3
+    out_ref[...] = s_ref[512:560, :] + s_ref[560:608, :]
+    sources = [out_ref.at[0:16], out_ref.at[16:32], zs_ref.at[0], out_ref.at[32:33]] + [zs_ref.at[1]] * 3
     targets = [sx, sy, sz.at[0], sxy, sz.at[1], sz.at[2], sz.at[3]]
     mass = [message(UPPER[i], sources[i], targets[i], s_send.at[i], s_recv.at[i]) for i in range(7)]
     start(mass[::-1])
+    own_rows()
     for c in range(4):
-        m_ref[c] = s_ref[0:256, 128 * c : 128 * c + 128].reshape(16, 2, 8, 128)
+        columns = slice(128 * c, 128 * c + 128)
+        m_ref[c] = (s_ref[0:256, columns] + s_ref[256:512, columns]).reshape(16, 2, 8, 128)
     receive(mass)
     for c in range(4):
         columns = slice(128 * c, 128 * c + 128)
@@ -422,6 +466,7 @@
         entries.append((mesh_step(z=a), z5.at[a], za.at[a]))
     ghost = numbered(entries, g_send, g_recv)
     start(ghost)
+    tables()
     receive(ghost)
 
     def tiles_of(zp, xz):
@@ -565,6 +610,7 @@
     targets = [fx, fy, fz.at[0], fxy, fz.at[1], fz.at[2], fz.at[3]]
     layer = [message(opposite(UPPER[i]), sources[i], targets[i], f_send.at[i], f_recv.at[i]) for i in range(7)]
     start(layer[::-1])
+    own_values()
     receive(layer)
     halo_ref[0:16] = fx[...].reshape(16, 128)
     halo_ref[16:32] = fy[...]
@@ -579,8 +625,12 @@
         uz_ref[272 + 8 * t : 280 + 8 * t] = jnp.broadcast_to(column, (8, 128))
     uz_ref[288:296] = jnp.where(sub == 0, fz[3], 0.0)
     uz_ref[296:304] = zero
-    for messages in (mass, ghost, *rounds, layer):
-        drain(messages)
+
+    def finish():
+        for messages in (mass, ghost, *rounds, layer):
+            drain(messages)
+
+    return finish
 
 
 FIELD = (16, 2, 8, 128)
@@ -597,8 +647,9 @@
 
 
 def kernel(sizes, data_hbm, cells_hbm, counts_hbm, u_ref, out_ref, *scratch):
-    (data_ref, cells_ref, counts_ref, send, recv, sent, d_ref, a0, b0, a1, b1, acc_ref, ov_ref,
-     l_ref, r_ref, halo_ref, uz_ref, val_ref, back_send, back_recv, back_sent,
+    a_refs, b_refs, scratch = scratch[:GROUPS], scratch[GROUPS : 2 * GROUPS], scratch[2 * GROUPS :]
+    (data_ref, cells_ref, counts_ref, send, recv, sent, d_ref, acc_ref, ov_ref, face_ref,
+     l_ref, r_ref, w_ref, part_ref, halo_ref, uz_ref, val_ref, back_send, back_recv, back_sent,
      in_sem, send_sem, recv_sem, *rest) = scratch
     here = position(sizes)
     me = (here[0] * sizes[1] + here[1]) * sizes[2] + here[2]
@@ -619,14 +670,19 @@
     greet(me, meanwhile)
     exchange_rows(me, send, recv, sent, send_sem.at[0], recv_sem.at[0])
     d_ref[...] = recv[...].T[: CAP * CHANNELS].reshape(CHANNELS, CAP, DEVICES)
-    splat_points(d_ref, acc_ref, ov_ref, a0, b0, a1, b1)
-    solve(sizes, here, acc_ref, ov_ref, u_ref, halo_ref, uz_ref, *rest)
-    interpolate(d_ref, u_ref, halo_ref, uz_ref, val_ref, l_ref, r_ref)
+    splat_outside(d_ref, acc_ref, ov_ref, a_refs, b_refs)
+    finish = solve(
+        sizes, here, lambda: splat_inside(acc_ref, a_refs, b_refs), lambda: interpolation_tables(d_ref, r_ref, w_ref),
+        lambda: interpolate_inside(u_ref, part_ref, l_ref, r_ref, w_ref),
+        acc_ref, ov_ref, face_ref, u_ref, halo_ref, uz_ref, *rest,
+    )
+    interpolate(halo_ref, uz_ref, part_ref, val_ref, l_ref, r_ref, w_ref)
     padded = jnp.concatenate([val_ref[...], jnp.zeros((DEVICES - CAP, DEVICES), F32)], axis=0)
     back_send[...] = padded.T
     exchange_rows(me, back_send, back_recv, back_sent, send_sem.at[1], recv_sem.at[1])
     slot = lax.broadcasted_iota(jnp.int32, (CAP, DEVICES), 0)
     out_ref[...] = jnp.where(slot < counts_ref[...], back_recv[...].T[:CAP], 0.0)
+    finish()
     pltpu.make_async_copy(send, recv, send_sem.at[0]).wait()
     pltpu.make_async_copy(back_send, back_recv, send_sem.at[1]).wait()
 
@@ -635,11 +691,11 @@
     data = jnp.transpose(point_data[0], (1, 2, 0))
     cells = jnp.transpose(point_cells[0], (1, 2, 0))
     dma = pltpu.SemaphoreType.DMA
-    shapes = [
+    shapes = [((608, POINTS), BF16)] * GROUPS + [((1040, POINTS), BF16)] * GROUPS + [
         ((7, CAP, DEVICES), F32), ((3, CAP, DEVICES), jnp.int32), ((1, DEVICES), jnp.int32),
         ((DEVICES, WIDTH), F32), ((DEVICES, WIDTH), F32), ((1, WIDTH), F32), ((CHANNELS, CAP, DEVICES), F32),
-        ((ROWS, 3 * POINTS), BF16), ((528, 3 * POINTS), BF16), ((ROWS, 3 * POINTS), BF16), ((528, 3 * POINTS), BF16),
-        ((ROWS, 512), F32), ((ROWS, 128), F32), ((ROWS, 512), BF16), ((512, POINTS), BF16),
+        ((608, 512), F32), ((608, 128), F32), ((48, 512), F32), ((ROWS, 512), BF16),
+        ((GROUPS, 512, POINTS), BF16), ((GROUPS, ROWS, POINTS), F32), ((GROUPS, 8, POINTS), F32),
         ((48, 128), F32), ((ROWS, 128), F32), ((CAP, DEVICES), F32),
         ((DEVICES, DEVICES), F32), ((DEVICES, DEVICES), F32), ((1, DEVICES), F32),
     ]
@@ -653,11 +709,31 @@
         + [pltpu.VMEM(s, F32) for s in SOLVE_SHAPES]
         + [dma((7,)), dma((7,)), dma((22,)), dma((22,)), dma((2, 24)), dma((2, 24)), dma((7,)), dma((7,))],
         compiler_params=pltpu.CompilerParams(
-            vmem_limit_bytes=24 * 1024 * 1024, collective_id=0, has_side_effects=True
+            vmem_limit_bytes=48 * 1024 * 1024, collective_id=0, has_side_effects=True
         ),
         name="reconstruct",
     )(*[pltpu.with_memory_space_constraint(v, pltpu.HBM) for v in (data, cells, send_counts)])
+    u, returned = pl.pallas_call(
+        put_out,
+        out_shape=[jax.ShapeDtypeStruct(s, F32) for s in (FIELD, (CAP, DEVICES))],
+        in_specs=[vmem()] * 2,
+        out_specs=[pl.BlockSpec(memory_space=pl.ANY)] * 2,
+        scratch_shapes=[dma((2,))],
+        compiler_params=pltpu.CompilerParams(vmem_limit_bytes=1024 * 1024),
+        name="put_out",
+    )(u, returned)
     return u.reshape(16, 16, 128), returned.T[None]
+
+
+def put_out(u_ref, value_ref, u_out, value_out, sems):
+    copies = [
+        pltpu.make_async_copy(u_ref, u_out, sems.at[0]),
+        pltpu.make_async_copy(value_ref, value_out, sems.at[1]),
+    ]
+    for copy in copies:
+        copy.start()
+    for copy in copies:
+        copy.wait()
 
 
 def solution(mesh):

time: 56.4 us -> 53.1 us (0.941)
  Pallas kernels: 54.4 us -> 52.3 us
  local copies, waits for them, and re-layouts: 1.26 us -> 0 us
    pallas_call x1, Pallas kernels: 54.4 us -> 51.6 us  [on_device(): pl.pallas_call(functools.partial(kernel, sizes), out_shape=[jax.ShapeDtyp...]
    unnamed x2 -> x0, local copies, waits for them, and re-layouts: 1.26 us -> none
    pallas_call x0 -> x1, Pallas kernels: none -> 0.68 us  [on_device(): pl.pallas_call(put_out, out_shape=[jax.ShapeDtypeStruct(s, F32) for s in...]
where the time goes in v4:
time: 53.1 us; the launch traced here: 52.9 us
  Pallas kernels  52.3 us (98%)
  between operations  0.64 us (1%)
    pallas_call x1, Pallas kernels, on_device(): pl.pallas_call(functools.partial(kernel, sizes), out_shape=[jax.ShapeDtyp...  51.6 us

profile of v4, /device:TPU:1, one launch (start us, length us, event | category | flops | bytes accessed | tf_op | source)
XLA Modules:
  0.0 52.9 jit_solution(4845393189130849238)
XLA Ops:
  0.6 51.6 %reconstruct.1 = (f32[16,2,8,128]{3,2,1,0:T(8,128)S(1)}, f32[32,128]{1,0:T(8,128)S(1)}) custom-call(f32[7,32,128]{2,1,0:T(8,128)} %bitcast.10, s32[3,32,128]{2,1,0:T(8,128)} %bitcast.11, s32[1,128]{1,0:T(1,128)} %counts_hbm.1), custom_call_target="tpu_custom_call" | custom-call | tf_op jit(solution)/shard_map/reconstruct/pallas_call | solution.py:702
  52.3 0.7 %put_out.1 = (f32[16,2,8,128]{3,2,1,0:T(8,128)}, f32[32,128]{1,0:T(8,128)}) custom-call(f32[16,2,8,128]{3,2,1,0:T(8,128)S(1)} %get-tuple-element.6.u_ref, f32[32,128]{1,0:T(8,128)S(1)} %get-tuple-element.7.value_ref), custom_call_target="tpu_custom_call" | custom-call | tf_op jit(solution)/shard_map/put_out/pallas_call | solution.py:716

commit v5 on v4

--- a/solution.py
+++ b/solution.py
@@ -108,7 +108,7 @@
     return lax.broadcasted_iota(jnp.int32, (16, WIDE), 0).astype(F32).astype(BF16)
 
 
-def build_block(d_ref, group, block, a_ref, b_ref):
+def build_block(d_ref, group, block, a_ref, b_ref, c_ref, x_ref):
     iota = tile_iota()
     zero = jnp.zeros((16, WIDE), BF16)
     lanes = slice(block * WIDE, (block + 1) * WIDE)
@@ -125,12 +125,6 @@
             for part in range(2):
                 value = jnp.where(z0, g0[c][part], jnp.where(z1, g1[c][part], zero))
                 b_ref[512 * part + 128 * c + 16 * t : 512 * part + 128 * c + 16 * t + 16, lanes] = value
-    top = bz == 127
-    both = zero
-    for c in range(4):
-        for part in range(2):
-            both = jnp.where(iota == c + 4 * part, g1[c][part], both)
-    b_ref[1024:1040, lanes] = jnp.where(top, both, zero)
     by, by1 = cy.astype(BF16), (cy + 1.0).astype(BF16)
     y0, y1 = by == iota, by1 == iota
     near, far = [], []
@@ -145,7 +139,7 @@
         for part in range(2):
             value = near[part] if below is None else jnp.where(below, far[part], zero)
             value = jnp.where(here, near[part], zero if below is None else value)
-            first = (256 * part + 16 * x) if x < 16 else 512 + 48 * part
+            first = (352 * part + 16 * x) if x < 16 else 256 + 48 * part
             a_ref[first : first + 16, lanes] = value
         below = here
     bx1 = (cx + 1.0).astype(BF16)
@@ -155,8 +149,26 @@
         at = iota + jnp.asarray(16 * t, BF16)
         x0, x1 = bx == at, bx1 == at
         for part in range(2):
-            first = 528 + 48 * part + 16 * t
+            first = 272 + 48 * part + 16 * t
             a_ref[first : first + 16, lanes] = jnp.where(x0, e0[part], jnp.where(x1, e1[part], zero))
+    x_near, x_far = split(1.0 - fx), split(fx)
+    for t in range(2):
+        at = iota + jnp.asarray(16 * t, BF16)
+        x0, x1 = bx == at, bx1 == at
+        for part in range(2):
+            first = 32 * part + 16 * t
+            x_ref[first : first + 16, lanes] = jnp.where(x0, x_near[part], jnp.where(x1, x_far[part], zero))
+    over = jnp.where(cz == 127.0, fz, 0.0)
+    over0, over1 = over * (1.0 - fy), over * fy
+    last = [zero, zero]
+    for c in range(4):
+        w0, w1 = split(v[c] * over0), split(v[c] * over1)
+        for part in range(2):
+            first = 80 * part + 16 * c
+            c_ref[first : first + 16, lanes] = jnp.where(y0, w0[part], jnp.where(y1, w1[part], zero))
+            last[part] = jnp.where(iota == c, w1[part], last[part])
+    for part in range(2):
+        c_ref[80 * part + 64 : 80 * part + 80, lanes] = jnp.where(by == 15, last[part], zero)
 
 
 ROW_DIMS = (((1,), (1,)), ((), ()))
@@ -166,32 +178,33 @@
     return lax.dot_general(left, right, ROW_DIMS, preferred_element_type=F32)
 
 
-def multiply_outside(piece, a_ref, b_ref, acc_ref, ov_ref):
+def multiply_outside(piece, a_ref, b_ref, c_ref, x_ref, acc_ref, ov_ref):
     if piece == 0:
-        acc_ref[512:608, 0:256] += rows_by_rows(a_ref[512:608, :], b_ref[0:256, :])
+        acc_ref[0:352, 0:256] += rows_by_rows(a_ref[0:352, :], b_ref[0:256, :])
     elif piece == 1:
-        acc_ref[512:608, 256:512] += rows_by_rows(a_ref[512:608, :], b_ref[256:512, :])
+        acc_ref[0:352, 256:512] += rows_by_rows(a_ref[0:352, :], b_ref[256:512, :])
     elif piece == 2:
-        acc_ref[512:560, :] += rows_by_rows(a_ref[512:560, :], b_ref[512:1024, :])
+        acc_ref[256:304, :] += rows_by_rows(a_ref[256:304, :], b_ref[512:1024, :])
     else:
-        ov_ref[:, 0:16] += rows_by_rows(a_ref[...], b_ref[1024:1040, :])
-
-
-def splat_outside(d_ref, acc_ref, ov_ref, a_refs, b_refs):
+        ov_ref[:, 0:64] += rows_by_rows(c_ref[...], x_ref[...])
+
+
+def splat_outside(d_ref, acc_ref, ov_ref, tiles):
     acc_ref[...] = jnp.zeros_like(acc_ref)
     ov_ref[...] = jnp.zeros_like(ov_ref)
-    for block in range(POINTS // WIDE):
-        build_block(d_ref, 0, block, a_refs[0], b_refs[0])
+    blocks = POINTS // WIDE
+    for block in range(blocks):
+        build_block(d_ref, 0, block, *tiles[0])
     for group in range(GROUPS):
-        for block in range(4):
-            if group + 1 < GROUPS and block < POINTS // WIDE:
-                build_block(d_ref, group + 1, block, a_refs[group + 1], b_refs[group + 1])
-            multiply_outside(block, a_refs[group], b_refs[group], acc_ref, ov_ref)
-
-
-def splat_inside(acc_ref, a_refs, b_refs):
-    for a_ref, b_ref in zip(a_refs, b_refs):
-        acc_ref[0:512, :] += rows_by_rows(a_ref[0:512, :], b_ref[0:512, :])
+        for piece in range(4):
+            if group + 1 < GROUPS and piece < blocks:
+                build_block(d_ref, group + 1, piece, *tiles[group + 1])
+            multiply_outside(piece, *tiles[group], acc_ref, ov_ref)
+
+
+def splat_inside(acc_ref, tiles):
+    for a_ref, b_ref, _, _ in tiles:
+        acc_ref[352:608, :] += rows_by_rows(a_ref[352:608, :], b_ref[0:512, :])
         acc_ref[0:256, :] += rows_by_rows(a_ref[0:256, :], b_ref[512:1024, :])
 
 
@@ -402,16 +415,21 @@
     lane, sub = grid_iotas()
     zero = jnp.zeros((8, 128), F32)
 
-    for part, tiles in ((0, 32), (1, 5)):
-        packed = zero
-        for i in range(tiles):
-            first = 512 * part + 8 * i
-            tile = ov_ref[pl.ds(first, 8), :] + ov_ref[pl.ds(first + (48 if part else 256), 8), :]
-            tile = tile + pltpu.roll(tile, 124, 1)
-            here_lanes = jnp.logical_and(lane >= 4 * i, lane < 4 * i + 4)
-            packed = jnp.where(here_lanes, roll_to(tile, 0, 4 * i), packed)
-        zs_ref[part] = packed
-    out_ref[...] = s_ref[512:560, :] + s_ref[560:608, :]
+    def over(first):
+        tile = ov_ref[pl.ds(first, 8), :] + ov_ref[pl.ds(first + 80, 8), :]
+        return tile + pltpu.roll(tile, 96, 1)
+
+    packed = zero
+    rest = roll_to(over(64), 0, 32)
+    for c in range(4):
+        for t in range(2):
+            tile = over(16 * c + 8 * t)
+            at = 32 * c + 16 * t
+            packed = jnp.where(jnp.logical_and(lane >= at, lane < at + 16), roll_to(tile, 0, at), packed)
+            rest = jnp.where(lane == 4 * t + c, roll_to(tile, 16, 4 * t + c), rest)
+    zs_ref[0] = packed
+    zs_ref[1] = rest
+    out_ref[...] = s_ref[256:304, :] + s_ref[304:352, :]
     sources = [out_ref.at[0:16], out_ref.at[16:32], zs_ref.at[0], out_ref.at[32:33]] + [zs_ref.at[1]] * 3
     targets = [sx, sy, sz.at[0], sxy, sz.at[1], sz.at[2], sz.at[3]]
     mass = [message(UPPER[i], sources[i], targets[i], s_send.at[i], s_recv.at[i]) for i in range(7)]
@@ -419,21 +437,20 @@
     own_rows()
     for c in range(4):
         columns = slice(128 * c, 128 * c + 128)
-        m_ref[c] = (s_ref[0:256, columns] + s_ref[256:512, columns]).reshape(16, 2, 8, 128)
+        m_ref[c] = (s_ref[0:256, columns] + s_ref[352:608, columns]).reshape(16, 2, 8, 128)
     receive(mass)
     for c in range(4):
         columns = slice(128 * c, 128 * c + 128)
         m_ref[c, 0] += sx[:, columns].reshape(2, 8, 128)
         from_y = sy[:, columns]
-        near_z = [roll_to(sz[2], 8 + 4 * t + c, 0) for t in range(2)]
         for x in range(16):
-            row = from_y[x : x + 1, :] + jnp.where(lane[0:1] == 0, near_z[x // 8][x % 8 : x % 8 + 1, :], 0.0)
+            row = from_y[x : x + 1, :] + jnp.where(lane == 0, roll_to(sz[2], 32 + x, 0), 0.0)[c : c + 1, :]
             m_ref[c, x, 0, 0:1, :] += row
         for i in range(32):
-            m_ref[c, i // 2, i % 2] += jnp.where(lane == 0, roll_to(sz[0], 4 * i + c, 0), 0.0)
+            m_ref[c, i // 2, i % 2] += jnp.where(lane == 0, roll_to(sz[0], 32 * c + 16 * (i % 2) + i // 2, 0), 0.0)
         for t in range(2):
             m_ref[c, 0, t] += jnp.where(lane == 0, roll_to(sz[1], 4 * t + c, 0), 0.0)
-        corner = sxy[:, columns] + jnp.where(lane[0:1] == 0, roll_to(sz[3], 16 + c, 0)[0:1], 0.0)
+        corner = sxy[:, columns] + jnp.where(lane == 0, roll_to(sz[3], 48, 0), 0.0)[c : c + 1, :]
         m_ref[c, 0, 0, 0:1, :] += corner
 
     def end(side, depth, size):
@@ -647,7 +664,7 @@
 
 
 def kernel(sizes, data_hbm, cells_hbm, counts_hbm, u_ref, out_ref, *scratch):
-    a_refs, b_refs, scratch = scratch[:GROUPS], scratch[GROUPS : 2 * GROUPS], scratch[2 * GROUPS :]
+    tiles, scratch = [scratch[i::GROUPS][:4] for i in range(GROUPS)], scratch[4 * GROUPS :]
     (data_ref, cells_ref, counts_ref, send, recv, sent, d_ref, acc_ref, ov_ref, face_ref,
      l_ref, r_ref, w_ref, part_ref, halo_ref, uz_ref, val_ref, back_send, back_recv, back_sent,
      in_sem, send_sem, recv_sem, *rest) = scratch
@@ -670,9 +687,9 @@
     greet(me, meanwhile)
     exchange_rows(me, send, recv, sent, send_sem.at[0], recv_sem.at[0])
     d_ref[...] = recv[...].T[: CAP * CHANNELS].reshape(CHANNELS, CAP, DEVICES)
-    splat_outside(d_ref, acc_ref, ov_ref, a_refs, b_refs)
+    splat_outside(d_ref, acc_ref, ov_ref, tiles)
     finish = solve(
-        sizes, here, lambda: splat_inside(acc_ref, a_refs, b_refs), lambda: interpolation_tables(d_ref, r_ref, w_ref),
+        sizes, here, lambda: splat_inside(acc_ref, tiles), lambda: interpolation_tables(d_ref, r_ref, w_ref),
         lambda: interpolate_inside(u_ref, part_ref, l_ref, r_ref, w_ref),
         acc_ref, ov_ref, face_ref, u_ref, halo_ref, uz_ref, *rest,
     )
@@ -691,10 +708,11 @@
     data = jnp.transpose(point_data[0], (1, 2, 0))
     cells = jnp.transpose(point_cells[0], (1, 2, 0))
     dma = pltpu.SemaphoreType.DMA
-    shapes = [((608, POINTS), BF16)] * GROUPS + [((1040, POINTS), BF16)] * GROUPS + [
+    tile_rows = (608, 1024, 160, 64)
+    shapes = [((rows, POINTS), BF16) for rows in tile_rows for _ in range(GROUPS)] + [
         ((7, CAP, DEVICES), F32), ((3, CAP, DEVICES), jnp.int32), ((1, DEVICES), jnp.int32),
         ((DEVICES, WIDTH), F32), ((DEVICES, WIDTH), F32), ((1, WIDTH), F32), ((CHANNELS, CAP, DEVICES), F32),
-        ((608, 512), F32), ((608, 128), F32), ((48, 512), F32), ((ROWS, 512), BF16),
+        ((608, 512), F32), ((160, 128), F32), ((48, 512), F32), ((ROWS, 512), BF16),
         ((GROUPS, 512, POINTS), BF16), ((GROUPS, ROWS, POINTS), F32), ((GROUPS, 8, POINTS), F32),
         ((48, 128), F32), ((ROWS, 128), F32), ((CAP, DEVICES), F32),
         ((DEVICES, DEVICES), F32), ((DEVICES, DEVICES), F32), ((1, DEVICES), F32),

time: 53.1 us -> 52 us (0.979)
  Pallas kernels: 52.3 us -> 51.2 us
    pallas_call x1, Pallas kernels: 51.6 us -> 50.5 us  [on_device(): pl.pallas_call(functools.partial(kernel, sizes), out_shape=[jax.ShapeDtyp...]
where the time goes in v5:
time: 52 us; the launch traced here: 51.9 us
  Pallas kernels  51.2 us (98%)
  between operations  0.64 us (1%)
    pallas_call x1, Pallas kernels, on_device(): pl.pallas_call(functools.partial(kernel, sizes), out_shape=[jax.ShapeDtyp...  50.5 us

profile of v5, /device:TPU:1, one launch (start us, length us, event | category | flops | bytes accessed | tf_op | source)
XLA Modules:
  0.0 51.9 jit_solution(11909816714622407925)
XLA Ops:
  0.6 50.5 %reconstruct.1 = (f32[16,2,8,128]{3,2,1,0:T(8,128)S(1)}, f32[32,128]{1,0:T(8,128)S(1)}) custom-call(f32[7,32,128]{2,1,0:T(8,128)} %bitcast.10, s32[3,32,128]{2,1,0:T(8,128)} %bitcast.11, s32[1,128]{1,0:T(1,128)} %counts_hbm.1), custom_call_target="tpu_custom_call" | custom-call | tf_op jit(solution)/shard_map/reconstruct/pallas_call | solution.py:720
  51.2 0.7 %put_out.1 = (f32[16,2,8,128]{3,2,1,0:T(8,128)}, f32[32,128]{1,0:T(8,128)}) custom-call(f32[16,2,8,128]{3,2,1,0:T(8,128)S(1)} %get-tuple-element.6.u_ref, f32[32,128]{1,0:T(8,128)S(1)} %get-tuple-element.7.value_ref), custom_call_target="tpu_custom_call" | custom-call | tf_op jit(solution)/shard_map/put_out/pallas_call | solution.py:734

commit v6 on v5

--- a/solution.py
+++ b/solution.py
@@ -43,23 +43,25 @@
     return pl.BlockSpec(memory_space=pltpu.VMEM)
 
 
+def far_first():
+    def hops(offset):
+        fields = (offset >> 5) & 3, (offset >> 3) & 3, offset & 3
+        return sum((0, 1, 2, 1)[field] for field in fields) + 0.5 * ((offset >> 2) & 1)
+
+    return sorted(range(1, DEVICES), key=lambda offset: (-hops(offset), offset * 37 % DEVICES))
+
+
 def greet(me, meanwhile):
     barrier = pltpu.get_barrier_semaphore()
-
-    @pl.loop(0, DEVICES - 8, step=8)
-    def _(step):
-        for q in range(8):
-            pl.semaphore_signal(barrier, inc=1, device_id=me ^ (step + q + 1), device_id_type=pl.DeviceIdType.LOGICAL)
-
-    for q in range(DEVICES - 7, DEVICES):
-        pl.semaphore_signal(barrier, inc=1, device_id=me ^ q, device_id_type=pl.DeviceIdType.LOGICAL)
+    for offset in far_first():
+        pl.semaphore_signal(barrier, inc=1, device_id=me ^ offset, device_id_type=pl.DeviceIdType.LOGICAL)
     meanwhile()
     pl.semaphore_wait(barrier, DEVICES - 1)
 
 
 def exchange_rows(me, send, recv, sent, send_sem, recv_sem):
-    def post(step):
-        other = me ^ ((step * 37) & (DEVICES - 1))
+    for offset in far_first():
+        other = me ^ offset
         pltpu.make_async_remote_copy(
             src_ref=send.at[pl.ds(other, 1)],
             dst_ref=recv.at[pl.ds(me, 1)],
@@ -68,14 +70,6 @@
             device_id=other,
             device_id_type=pl.DeviceIdType.LOGICAL,
         ).start()
-
-    @pl.loop(0, DEVICES - 8, step=8)
-    def _(step):
-        for q in range(8):
-            post(step + q + 1)
-
-    for q in range(DEVICES - 7, DEVICES):
-        post(q)
     pltpu.make_async_copy(send.at[pl.ds(me, 1)], recv.at[pl.ds(me, 1)], recv_sem).start()
     pltpu.make_async_copy(send.at[pl.ds(me, 1)], sent, send_sem).start()
     pltpu.make_async_copy(send, recv, recv_sem).wait()
@@ -98,9 +92,18 @@
 WIDE = 256
 
 
-def lane_rows(d_ref, group, block, channels):
+def tile(value):
+    return jnp.concatenate([value, value], axis=0).astype(BF16)
+
+
+def split_tile(value):
+    high = tile(value)
+    return high, tile(value - high[0:8].astype(F32))
+
+
+def lane_rows(d_ref, group, block, channels, rows):
     first = (group * POINTS + block * WIDE) // DEVICES
-    wide = lambda c, q: jnp.broadcast_to(d_ref[c, pl.ds(first + q, 1), :], (16, DEVICES))
+    wide = lambda c, q: jnp.broadcast_to(d_ref[c, pl.ds(first + q, 1), :], (rows, DEVICES))
     return [jnp.concatenate([wide(c, q) for q in range(WIDE // DEVICES)], axis=1) for c in channels]
 
 
@@ -112,12 +115,12 @@
     iota = tile_iota()
     zero = jnp.zeros((16, WIDE), BF16)
     lanes = slice(block * WIDE, (block + 1) * WIDE)
-    v = lane_rows(d_ref, group, block, range(4))
-    fx, fy, fz, cx, cy, cz = lane_rows(d_ref, group, block, range(4, 10))
-    bz = cz.astype(BF16)
-    bz1 = (cz + 1.0).astype(BF16)
-    g0 = [split(v[c] * (1.0 - fz)) for c in range(4)]
-    g1 = [split(v[c] * fz) for c in range(4)]
+    v = lane_rows(d_ref, group, block, range(4), 8)
+    fx, fy, fz, cx, cy, cz = lane_rows(d_ref, group, block, range(4, 10), 8)
+    bz = tile(cz)
+    bz1 = tile(cz + 1.0)
+    g0 = [split_tile(v[c] * (1.0 - fz)) for c in range(4)]
+    g1 = [split_tile(v[c] * fz) for c in range(4)]
     for t in range(8):
         at = iota + jnp.asarray(16 * t, BF16)
         z0, z1 = bz == at, bz1 == at
@@ -125,14 +128,14 @@
             for part in range(2):
                 value = jnp.where(z0, g0[c][part], jnp.where(z1, g1[c][part], zero))
                 b_ref[512 * part + 128 * c + 16 * t : 512 * part + 128 * c + 16 * t + 16, lanes] = value
-    by, by1 = cy.astype(BF16), (cy + 1.0).astype(BF16)
+    by, by1 = tile(cy), tile(cy + 1.0)
     y0, y1 = by == iota, by1 == iota
     near, far = [], []
     for along, out in ((1.0 - fx, near), (fx, far)):
-        w0, w1 = split(along * (1.0 - fy)), split(along * fy)
+        w0, w1 = split_tile(along * (1.0 - fy)), split_tile(along * fy)
         for part in range(2):
             out.append(jnp.where(y0, w0[part], jnp.where(y1, w1[part], zero)))
-    bx = cx.astype(BF16)
+    bx = tile(cx)
     below = None
     for x in range(17):
         here = bx == x
@@ -142,16 +145,16 @@
             first = (352 * part + 16 * x) if x < 16 else 256 + 48 * part
             a_ref[first : first + 16, lanes] = value
         below = here
-    bx1 = (cx + 1.0).astype(BF16)
+    bx1 = tile(cx + 1.0)
     edge = jnp.where(cy == 15.0, fy, 0.0)
-    e0, e1 = split((1.0 - fx) * edge), split(fx * edge)
+    e0, e1 = split_tile((1.0 - fx) * edge), split_tile(fx * edge)
     for t in range(2):
         at = iota + jnp.asarray(16 * t, BF16)
         x0, x1 = bx == at, bx1 == at
         for part in range(2):
             first = 272 + 48 * part + 16 * t
             a_ref[first : first + 16, lanes] = jnp.where(x0, e0[part], jnp.where(x1, e1[part], zero))
-    x_near, x_far = split(1.0 - fx), split(fx)
+    x_near, x_far = split_tile(1.0 - fx), split_tile(fx)
     for t in range(2):
         at = iota + jnp.asarray(16 * t, BF16)
         x0, x1 = bx == at, bx1 == at
@@ -162,7 +165,7 @@
     over0, over1 = over * (1.0 - fy), over * fy
     last = [zero, zero]
     for c in range(4):
-        w0, w1 = split(v[c] * over0), split(v[c] * over1)
+        w0, w1 = split_tile(v[c] * over0), split_tile(v[c] * over1)
         for part in range(2):
             first = 80 * part + 16 * c
             c_ref[first : first + 16, lanes] = jnp.where(y0, w0[part], jnp.where(y1, w1[part], zero))
@@ -218,7 +221,7 @@
         r_ref[group, 400:512, :] = jnp.zeros((112, POINTS), BF16)
         for block in range(POINTS // WIDE):
             lanes = slice(block * WIDE, (block + 1) * WIDE)
-            fx, fy, fz, cx, cy, cz = lane_rows(d_ref, group, block, range(4, 10))
+            fx, fy, fz, cx, cy, cz = lane_rows(d_ref, group, block, range(4, 10), 16)
             bz, bz1 = cz.astype(BF16), (cz + 1.0).astype(BF16)
             g0, g1 = split(1.0 - fz), split(fz)
             for t in range(8):
@@ -332,6 +335,26 @@
     return total + comb(*sides).reshape(n, 2, 8, 128)
 
 
+def own_star(comb, along_x, along_y, along_z):
+    nothing = jnp.zeros((8, 128), F32)
+    end_slab = jnp.zeros((1, 2, 8, 128), F32)
+    wide = jnp.concatenate([end_slab, along_x, end_slab], axis=0)
+    return slab_star(comb, wide, along_y, along_z, lambda side, i: nothing, lambda side, i, t: nothing)
+
+
+def add_outside(total, low_sign, x_low, x_high, rows, tiles):
+    sub3 = lax.broadcasted_iota(jnp.int32, (16, 8, 128), 1)
+    lanes = lax.broadcasted_iota(jnp.int32, (32, 8, 128), 2)
+    edge = [jnp.stack([rows(side, i + 1) for i in range(16)]) for side in range(2)]
+    along_y = jnp.stack([jnp.where(sub3 == 0, low_sign * edge[0], 0.0), jnp.where(sub3 == 7, edge[1], 0.0)], axis=1)
+    edge = [jnp.stack([tiles(side, i + 1, t) for i in range(16) for t in range(2)]) for side in range(2)]
+    along_z = jnp.where(lanes == 0, low_sign * edge[0], jnp.where(lanes == 127, edge[1], 0.0))
+    total = total + (along_y + along_z.reshape(16, 2, 8, 128))
+    return jnp.concatenate(
+        [total[0:1] + low_sign * x_low[None], total[1:15], total[15:16] + x_high[None]], axis=0
+    )
+
+
 def layer_star_y(comb, side, fx, fy, fz):
     row = lax.broadcasted_iota(jnp.int32, (16, 128), 0)
     lane16 = lax.broadcasted_iota(jnp.int32, (16, 128), 1)
@@ -374,7 +397,7 @@
     sizes, here, own_rows, tables, own_values, s_ref, ov_ref, out_ref, u_ref, halo_ref, uz_ref,
     m_ref, zs_ref, sx, sy, sxy, sz,
     z5, xa, xb, ya, yb, exy, za, exz, eyz,
-    pw, rw, z3, px, rx, py, py2, ry, pxy, pz, pxz, pyz, inv_ref, diag_ref, plane_ref, uzp,
+    pw, rw, z3, px, rx, py, py2, ry, pxy, pz, pxz, pyz, inv_ref, diag_ref, plane_ref, uzp, pre_ref,
     fx, fy, fxy, fz, s_send, s_recv, g_send, g_recv, h_send, h_recv, f_send, f_recv,
 ):
     lower = [here[a] > 0 for a in range(3)]
@@ -465,6 +488,12 @@
     def numbered(entries, send, recv):
         return [message(step, a, b, send.at[i], recv.at[i]) for i, (step, a, b) in enumerate(entries)]
 
+    def difference(low, high):
+        return high - low
+
+    def plus(low, high):
+        return low + high
+
     for side in range(2):
         for i, (c, depth) in enumerate(((0, 0), (2, 0), (1, 0), (3, 0), (2, 1))):
             z5[side, i] = pack(lambda k, c=c: m_ref[c, k // 2, k % 2], end(side, depth, 128))
@@ -483,6 +512,7 @@
         entries.append((mesh_step(z=a), z5.at[a], za.at[a]))
     ghost = numbered(entries, g_send, g_recv)
     start(ghost)
+    pre_ref[...] = own_star(difference, m_ref[0], m_ref[1], m_ref[2])
     tables()
     receive(ghost)
 
@@ -507,12 +537,6 @@
 
     def grid2(get):
         return [[get(a, b) for b in range(2)] for a in range(2)]
-
-    def difference(low, high):
-        return high - low
-
-    def plus(low, high):
-        return low + high
 
     nx = {
         "plane": both(lambda a: ya[a, 0]), "xy": grid2(lambda a, b: exy[a, b, 0:1]),
@@ -526,12 +550,22 @@
         "plane": both(lambda a: ya[a, 2]), "yz": grid2(lambda a, b: eyz[a, b, 0]),
         "zp2": both(lambda a: za[a, 4]), "own_z": both(lambda a: z5[1 - a, 1]),
     }
-    along_x = jnp.concatenate([xa[0], m_ref[0], xa[1]], axis=0)
-    along_y = jnp.concatenate([xb[0, 0:1], m_ref[1], xb[1, 0:1]], axis=0)
-    along_z = jnp.concatenate([xb[0, 1:2], m_ref[2], xb[1, 1:2]], axis=0)
     rows = rows_of(lambda side, x: ya[side, 1, x : x + 1, :], grid2(lambda a, b: exy[a, b, 1:2]))
     tiles = tiles_of(both(lambda a: za[a, 1]), grid2(lambda a, b: exz[a, b, 1]))
-    source = -0.5 * slab_star(difference, along_x, along_y, along_z, rows, tiles)
+
+    def end_star(comb, a, three, along_y, along_z, rows, tiles):
+        at = 17 * a
+        return slab_star(
+            comb, jnp.stack(three), along_y[None], along_z[None],
+            lambda side, i: rows(side, at), lambda side, i, t: tiles(side, at, t),
+        )
+
+    ends = [
+        end_star(difference, 0, [xa[0, 0], xa[0, 1], m_ref[0, 0]], xb[0, 0], xb[0, 1], rows, tiles),
+        end_star(difference, 1, [m_ref[0, 15], xa[1, 0], xa[1, 1]], xb[1, 0], xb[1, 1], rows, tiles),
+    ]
+    inside = add_outside(pre_ref[...], -1.0, xa[0, 1], xa[1, 0], rows, tiles)
+    source = -0.5 * jnp.concatenate([ends[0], inside, ends[1]], axis=0)
 
     def shift_diagonal(mass_part):
         return 6.0 + base_screen + point_screen * mass_part
@@ -595,6 +629,8 @@
         rounds.append(ghosts)
         start(ghosts)
         u_ref[...] += following
+        own = pw[e]
+        pre_ref[...] = rw[e] - (diag_ref[1:17] * own - own_star(plus, own, own, own))
         receive(ghosts)
         p = {
             "plane": both(lambda a: py[e, a]), "plane2": both(lambda a: py2[e, a]),
@@ -603,12 +639,15 @@
             "own_z": both(lambda a: z3[e, 1 - a, 0]),
             "xz": grid2(lambda a, b: pxz[e, a, b]), "yz": grid2(lambda a, b: pyz[e, a, b]),
         }
-        wide = jnp.concatenate([px[e, 0], pw[e], px[e, 1]], axis=0)
-        middle = wide[1:19]
         rows = rows_of(lambda side, x: py[e, side, x : x + 1, :], p["xy"])
-        around = slab_star(plus, wide, middle, middle, rows, tiles_of(p["zp"], p["xz"]))
-        residual = jnp.concatenate([rx[e, 0][None], rw[e], rx[e, 1][None]], axis=0)
-        residual = residual - (diag_ref[...] * middle - around)
+        tiles = tiles_of(p["zp"], p["xz"])
+        inside = add_outside(pre_ref[...], 1.0, px[e, 0, 1], px[e, 1, 0], rows, tiles)
+        ends = []
+        for a, three in enumerate(([px[e, 0, 0], px[e, 0, 1], pw[e, 0]], [pw[e, 15], px[e, 1, 0], px[e, 1, 1]])):
+            around = end_star(plus, a, three, three[1], three[1], rows, tiles)
+            ends.append(rx[e, a][None] - (diag_ref[17 * a][None] * three[1][None] - around))
+        middle = jnp.concatenate([px[e, 0, 1][None], pw[e], px[e, 1, 0][None]], axis=0)
+        residual = jnp.concatenate([ends[0], inside, ends[1]], axis=0)
         keep, push = factors[2 * e + 1]
         slabs = keep * middle + push * (residual * inv_ref[...])
 
@@ -657,10 +696,10 @@
     (2, 5, 8, 128), (2, 2, 2, 8, 128), (2, 2, 2, 8, 128),
     (2, *FIELD), (2, *FIELD), (2, 2, 3, 8, 128), (2, 2, 2, 2, 8, 128), (2, 2, 2, 8, 128),
     (2, 2, 16, 128), (2, 2, 16, 128), (2, 2, 16, 128), (2, 2, 2, 1, 128), (2, 2, 3, 8, 128),
-    (2, 2, 2, 8, 128), (2, 2, 2, 8, 128), (18, 2, 8, 128), (18, 2, 8, 128), (3, 2, 16, 128), (8, 128),
+    (2, 2, 2, 8, 128), (2, 2, 2, 8, 128), (18, 2, 8, 128), (18, 2, 8, 128), (3, 2, 16, 128), (8, 128), FIELD,
     (2, 8, 128), (16, 128), (1, 128), (4, 8, 128),
 ]
-LANDING = [2, 3, 4, 5, 7, 8, 9, 10, 11, 12, 13, 14, 18, 19, 20, 21, 22, 23, 24, 25, 26, 31, 32, 33, 34]
+LANDING = [2, 3, 4, 5, 7, 8, 9, 10, 11, 12, 13, 14, 18, 19, 20, 21, 22, 23, 24, 25, 26, 32, 33, 34, 35]
 
 
 def kernel(sizes, data_hbm, cells_hbm, counts_hbm, u_ref, out_ref, *scratch):

time: 52 us -> 49.7 us (0.956)
  Pallas kernels: 51.2 us -> 48.8 us
    pallas_call x1, Pallas kernels: 50.5 us -> 48.2 us  [on_device(): pl.pallas_call(functools.partial(kernel, sizes), out_shape=[jax.ShapeDtyp...]
where the time goes in v6:
time: 49.7 us; the launch traced here: 49.6 us
  Pallas kernels  48.8 us (98%)
  between operations  0.8 us (2%)
    pallas_call x1, Pallas kernels, on_device(): pl.pallas_call(functools.partial(kernel, sizes), out_shape=[jax.ShapeDtyp...  48.2 us

profile of v6, /device:TPU:1, one launch (start us, length us, event | category | flops | bytes accessed | tf_op | source)
XLA Modules:
  0.0 49.6 jit_solution(11341174913986857525)
XLA Ops:
  0.6 48.2 %reconstruct.1 = (f32[16,2,8,128]{3,2,1,0:T(8,128)S(1)}, f32[32,128]{1,0:T(8,128)S(1)}) custom-call(f32[7,32,128]{2,1,0:T(8,128)} %bitcast.10, s32[3,32,128]{2,1,0:T(8,128)} %bitcast.11, s32[1,128]{1,0:T(1,128)} %counts_hbm.1), custom_call_target="tpu_custom_call" | custom-call | tf_op jit(solution)/shard_map/reconstruct/pallas_call | solution.py:759
  48.8 0.7 %put_out.1 = (f32[16,2,8,128]{3,2,1,0:T(8,128)}, f32[32,128]{1,0:T(8,128)}) custom-call(f32[16,2,8,128]{3,2,1,0:T(8,128)S(1)} %get-tuple-element.6.u_ref, f32[32,128]{1,0:T(8,128)S(1)} %get-tuple-element.7.value_ref), custom_call_target="tpu_custom_call" | custom-call | tf_op jit(solution)/shard_map/put_out/pallas_call | solution.py:773

commit v7 on v6

--- a/solution.py
+++ b/solution.py
@@ -193,8 +193,6 @@
 
 
 def splat_outside(d_ref, acc_ref, ov_ref, tiles):
-    acc_ref[...] = jnp.zeros_like(acc_ref)
-    ov_ref[...] = jnp.zeros_like(ov_ref)
     blocks = POINTS // WIDE
     for block in range(blocks):
         build_block(d_ref, 0, block, *tiles[0])
@@ -263,9 +261,9 @@
 def interpolate_inside(u_ref, part_ref, l_ref, r_ref, w_ref):
     high_and_low(l_ref, 0, u_ref[...].reshape(256, 128))
 
-    @pl.loop(0, GROUPS, step=4)
+    @pl.loop(0, GROUPS, step=8)
     def _(first):
-        for step in range(4):
+        for step in range(8):
             group = first + step
             g = jnp.dot(l_ref[0:256, 0:384], r_ref[group, 0:384], preferred_element_type=F32)
             part_ref[group] = weighted(g, w_ref, group, 0)
@@ -279,9 +277,9 @@
     low = jnp.where(lane == 1, top - high, 0.0)
     l_ref[:, 384:512] = jnp.where(jnp.logical_or(lane == 0, lane == 2), high, low).astype(BF16)
 
-    @pl.loop(0, GROUPS, step=4)
+    @pl.loop(0, GROUPS, step=8)
     def _(first):
-        for step in range(4):
+        for step in range(8):
             group = first + step
             g = jnp.dot(l_ref[256:ROWS, :], r_ref[group], preferred_element_type=F32)
             total = part_ref[group] + weighted(g, w_ref, group, 256)
@@ -722,6 +720,8 @@
         for load in loads:
             load.wait()
         prepare_rows(data_ref, cells_ref, counts_ref, send)
+        acc_ref[...] = jnp.zeros_like(acc_ref)
+        ov_ref[...] = jnp.zeros_like(ov_ref)
 
     greet(me, meanwhile)
     exchange_rows(me, send, recv, sent, send_sem.at[0], recv_sem.at[0])

time: 49.7 us -> 49.5 us (level)
  no operation moved by 1% of the time
where the time goes in v7:
time: 49.5 us; the launch traced here: 49.4 us
  Pallas kernels  48.6 us (98%)
  between operations  0.8 us (2%)
    pallas_call x1, Pallas kernels, on_device(): pl.pallas_call(functools.partial(kernel, sizes), out_shape=[jax.ShapeDtyp...  47.9 us

profile of v7, /device:TPU:1, one launch (start us, length us, event | category | flops | bytes accessed | tf_op | source)
XLA Modules:
  0.0 49.4 jit_solution(17607751058116940016)
XLA Ops:
  0.6 47.9 %reconstruct.1 = (f32[16,2,8,128]{3,2,1,0:T(8,128)S(1)}, f32[32,128]{1,0:T(8,128)S(1)}) custom-call(f32[7,32,128]{2,1,0:T(8,128)} %bitcast.10, s32[3,32,128]{2,1,0:T(8,128)} %bitcast.11, s32[1,128]{1,0:T(1,128)} %counts_hbm.1), custom_call_target="tpu_custom_call" | custom-call | tf_op jit(solution)/shard_map/reconstruct/pallas_call | solution.py:759
  48.6 0.7 %put_out.1 = (f32[16,2,8,128]{3,2,1,0:T(8,128)}, f32[32,128]{1,0:T(8,128)}) custom-call(f32[16,2,8,128]{3,2,1,0:T(8,128)S(1)} %get-tuple-element.6.u_ref, f32[32,128]{1,0:T(8,128)S(1)} %get-tuple-element.7.value_ref), custom_call_target="tpu_custom_call" | custom-call | tf_op jit(solution)/shard_map/put_out/pallas_call | solution.py:773

commit v8 on v7

--- a/solution.py
+++ b/solution.py
@@ -707,14 +707,14 @@
      in_sem, send_sem, recv_sem, *rest) = scratch
     here = position(sizes)
     me = (here[0] * sizes[1] + here[1]) * sizes[2] + here[2]
-    for at in LANDING:
-        rest[at][...] = jnp.zeros(rest[at].shape, F32)
     loads = [
         pltpu.make_async_copy(source, target, in_sem.at[i])
         for i, (source, target) in enumerate(((data_hbm, data_ref), (cells_hbm, cells_ref), (counts_hbm, counts_ref)))
     ]
     for load in loads:
         load.start()
+    for at in LANDING:
+        rest[at][...] = jnp.zeros(rest[at].shape, F32)
 
     def meanwhile():
         for load in loads:

time: 49.5 us -> 49.5 us (level)
  no operation moved by 1% of the time
where the time goes in v8:
time: 49.5 us; the launch traced here: 49.4 us
  Pallas kernels  48.6 us (98%)
  between operations  0.8 us (2%)
    pallas_call x1, Pallas kernels, on_device(): pl.pallas_call(functools.partial(kernel, sizes), out_shape=[jax.ShapeDtyp...  47.9 us

profile of v8, /device:TPU:1, one launch (start us, length us, event | category | flops | bytes accessed | tf_op | source)
XLA Modules:
  0.0 49.4 jit_solution(16401675713946057392)
XLA Ops:
  0.6 47.9 %reconstruct.1 = (f32[16,2,8,128]{3,2,1,0:T(8,128)S(1)}, f32[32,128]{1,0:T(8,128)S(1)}) custom-call(f32[7,32,128]{2,1,0:T(8,128)} %bitcast.10, s32[3,32,128]{2,1,0:T(8,128)} %bitcast.11, s32[1,128]{1,0:T(1,128)} %counts_hbm.1), custom_call_target="tpu_custom_call" | custom-call | tf_op jit(solution)/shard_map/reconstruct/pallas_call | solution.py:759
  48.6 0.7 %put_out.1 = (f32[16,2,8,128]{3,2,1,0:T(8,128)}, f32[32,128]{1,0:T(8,128)}) custom-call(f32[16,2,8,128]{3,2,1,0:T(8,128)S(1)} %get-tuple-element.6.u_ref, f32[32,128]{1,0:T(8,128)S(1)} %get-tuple-element.7.value_ref), custom_call_target="tpu_custom_call" | custom-call | tf_op jit(solution)/shard_map/put_out/pallas_call | solution.py:773
